TPU v7x, 512 devices: a whole 4x8x8 slice. The times are simulated.
512 devices in a mesh: ch: 64 (over z_hi, y, core), freq: 8 (over z_lo, x).
Axes of the slice: x: 4, y: 8, z: 8 (z_hi: 4, z_lo: 2; z = z_hi * 2 + z_lo), core: 2. Of those that a mesh axis runs over, the one named last changes fastest.
Arguments:
- strain: bfloat16 [2048, 8, 2048], P('ch'), may hold values from -100 to 100
- channel_ok: int32 [2048], P('ch'), may hold values 0 or 1
- window_ok: int32 [2048, 8], P('ch'), may hold values 0 or 1
Outputs:
- stack_ahead: bfloat16 [2, 256, 2048, 128], P(None, 'freq', 'ch')
- stack_behind: bfloat16 [2, 256, 2048, 128], P(None, 'freq', 'ch')
All inputs are finite; a program needn't handle non-finite values. No bound on the sum of `channel_ok` or of `window_ok` on one device may be relied on, other than what follows from the above.
Results may differ from a plain program's by a relative error of at most 0.0082.
Values may be sent and summed in bfloat16 or wider, within the bound.
A program may use at most 64 MiB of HBM per device.

v0:
```python
import math

import jax
import jax.numpy as jnp
from jax import lax
from jax.sharding import PartitionSpec as P

WINDOWS = 8
SAMPLES = 2048
BINS = 256
REACH = 128
TIME_HALF = 128
BIN_HALF = 32
AHEAD = 4


def extended(block, sides, width):
    for axis, dim in sides:
        count = lax.axis_size(axis)
        forward = [(i, i + 1) for i in range(count - 1)]
        backward = [(target, source) for source, target in forward]
        low = lax.ppermute(
            lax.slice_in_dim(block, block.shape[dim] - width, None, axis=dim), axis, forward
        )
        high = lax.ppermute(lax.slice_in_dim(block, 0, width, axis=dim), axis, backward)
        block = jnp.concatenate([low, block, high], axis=dim)
    return block


def from_behind(value, axis, by):
    peers = lax.axis_size(axis)
    pairs = [(i, i + by) for i in range(peers) if 0 <= i + by < peers]
    return lax.ppermute(value, axis, pairs)


def skew_take(dense_mat, offset, reach_cols):
    leading = dense_mat.shape[:-2]
    row_count = dense_mat.shape[-2]
    col_count = dense_mat.shape[-1]
    flattened = dense_mat.reshape(leading + (row_count * col_count,))[..., offset:]
    widths = [(0, 0)] * len(leading) + [(0, row_count + offset)]
    flattened = jnp.pad(flattened, widths)
    return flattened.reshape(leading + (row_count, col_count + 1))[..., :reach_cols]


def dft_table(first_bin, bin_count):
    bin_freq = first_bin + 1 + lax.iota(jnp.int32, bin_count)
    sample_ids = lax.iota(jnp.int32, SAMPLES)
    phase = (bin_freq[:, None] * sample_ids[None, :] % SAMPLES).astype(jnp.float32) * (
        2.0 * math.pi / SAMPLES
    )
    norm_scale = 1.0 / math.sqrt(SAMPLES)
    return jnp.stack([jnp.cos(phase) * norm_scale, -jnp.sin(phase) * norm_scale], axis=1).astype(
        jnp.bfloat16
    )


def level_windows(samples_in):
    channels, count, length = samples_in.shape
    block = 2 * TIME_HALF
    piece_count = length // block
    magnitude = jnp.abs(samples_in).reshape(channels, count, piece_count, block)
    zero_block = jnp.zeros_like(magnitude[:, :, :1])
    previous = jnp.concatenate([zero_block, magnitude[:, :, :-1]], axis=2)
    following = jnp.concatenate([magnitude[:, :, 1:], zero_block], axis=2)
    widened = jnp.concatenate([previous, magnitude, following], axis=3)
    source_ids = lax.iota(jnp.int32, 3 * block)[:, None] - block
    target_ids = lax.iota(jnp.int32, block)[None, :]
    window_ones = (jnp.abs(source_ids - target_ids) <= TIME_HALF).astype(jnp.bfloat16)
    window_sums = jnp.einsum(
        "cwnp,pq->cwnq", widened, window_ones, preferred_element_type=jnp.float32
    )
    level_mean = window_sums.reshape(channels, count, length) / (2 * TIME_HALF + 1)
    return (samples_in.astype(jnp.float32) / (level_mean + 1e-06)).astype(jnp.bfloat16)


def cross_terms(white_flat, usable_b, partners, partner_usable):
    bin_count = white_flat.shape[0]
    channels = usable_b.shape[0]
    left_rows = white_flat.reshape(bin_count, channels, 2 * WINDOWS)
    sign_flip = jnp.concatenate(
        [jnp.ones((WINDOWS,), jnp.bfloat16), -jnp.ones((WINDOWS,), jnp.bfloat16)]
    )
    left_conj = left_rows * sign_flip
    joined = jnp.concatenate(partners, axis=1).reshape(bin_count, -1, 2, WINDOWS)
    right_same = joined.reshape(bin_count, -1, 2 * WINDOWS)
    right_swap = jnp.flip(joined, axis=2).reshape(bin_count, -1, 2 * WINDOWS)
    real_part = jnp.einsum(
        "kiv,kjv->kij", left_rows, right_same, preferred_element_type=jnp.float32
    )
    imag_part = jnp.einsum(
        "kiv,kjv->kij", left_conj, right_swap, preferred_element_type=jnp.float32
    )
    counts = jnp.dot(
        usable_b, jnp.concatenate(partner_usable, axis=0).T, preferred_element_type=jnp.float32
    )
    return (real_part, imag_part, counts)


def stacks_from(real_part, imag_part, counts, offset):
    divisor = jnp.maximum(skew_take(counts, offset, REACH), 1.0)
    stacked = jnp.stack(
        [
            skew_take(real_part, offset, REACH) / divisor,
            skew_take(imag_part, offset, REACH) / divisor,
        ]
    )
    return stacked.astype(jnp.bfloat16)


def per_device(strain, channel_ok, window_ok):
    channels = strain.shape[0]
    freq_devices = lax.axis_size("freq")
    bin_count = BINS // freq_devices
    freq_index = lax.axis_index("freq")
    spectra = jnp.einsum(
        "kps,cws->kcpw",
        dft_table(freq_index * bin_count, bin_count),
        level_windows(strain),
        preferred_element_type=jnp.float32,
    )
    band_power = spectra[:, :, 0] * spectra[:, :, 0] + spectra[:, :, 1] * spectra[:, :, 1]
    band_power = band_power.reshape(bin_count, channels * WINDOWS)
    padded = extended(band_power.astype(jnp.bfloat16), (("freq", 0),), BIN_HALF).astype(
        band_power.dtype
    )
    row_ids = lax.iota(jnp.int32, bin_count)[:, None] + BIN_HALF
    col_ids = lax.iota(jnp.int32, bin_count + 2 * BIN_HALF)[None, :]
    smoother_ones = (jnp.abs(col_ids - row_ids) <= BIN_HALF).astype(jnp.float32)
    smooth = jnp.dot(
        smoother_ones, padded, precision=lax.Precision.HIGHEST, preferred_element_type=jnp.float32
    ) / (2 * BIN_HALF + 1)
    inverse = (1.0 / jnp.sqrt(smooth + 1e-06)).reshape(bin_count, channels, 1, WINDOWS)
    usable = (channel_ok[:, None] * window_ok).astype(jnp.float32)
    white = (spectra * inverse * usable[None, :, None, :]).astype(jnp.bfloat16)
    white_flat = white.reshape(bin_count, channels * 2 * WINDOWS)
    usable_b = usable.astype(jnp.bfloat16)
    ahead_flat = [white_flat]
    ahead_usable = [usable_b]
    for distance in range(1, AHEAD + 1):
        arrived = from_behind((white_flat, usable_b), "ch", -distance)
        ahead_flat.append(arrived[0])
        ahead_usable.append(arrived[1])
    real_part, imag_part, counts = cross_terms(white_flat, usable_b, ahead_flat, ahead_usable)
    stack_ahead = stacks_from(real_part, imag_part, counts, 1)
    behind_offset = AHEAD * channels - REACH
    received = []
    for distance in range(AHEAD, 0, -1):
        received.append(from_behind(stack_ahead, "ch", distance))
    received.append(stack_ahead)
    joined = jnp.concatenate(received, axis=2)
    turned = jnp.flip(jnp.swapaxes(joined, 2, 3), axis=2)
    picked = jnp.flip(skew_take(turned, behind_offset, channels), axis=2)
    conj_sign = jnp.array([1.0, -1.0], jnp.bfloat16).reshape(2, 1, 1, 1)
    stack_behind = jnp.swapaxes(picked, 2, 3) * conj_sign
    return (stack_ahead, stack_behind)


def solution(mesh):
    placed = (P("ch", None, None), P("ch"), P("ch", None))
    return jax.shard_map(
        per_device,
        mesh=mesh,
        in_specs=placed,
        out_specs=(P(None, "freq", "ch", None), P(None, "freq", "ch", None)),
        check_vma=False,
    )
```

profile of v0, /device:TPU:384, one launch (start us, length us, event | category | flops | bytes accessed | tf_op | source)
XLA Modules:
  0.0 268.8 jit_solution(890099350847224583)
XLA Ops:
  0.6 0.7 fusion.56
  1.3 4.8 %collective-permute-start.6 = (bf16[32,8]{0,1:T(8,128)(2,1)S(1)}, bf16[32,8]{0,1:T(8,128)(2,1)S(1)}, u32[]{:S(2)}, u32[]{:S(2)}) collective-permute-start(bf16[32,8]{0,1:T(8,128)(2,1)S(1)} %get-tuple-element.6), channel_id=1, source_target_pairs={{8,0},{16,8},{24,16},{32,24},{40,32},{48,40},{56,48},{64,56},{72,6... | collective-permute-start | bytes 1544 | tf_op jit(solution)/shard_map/ppermute | solution.py:33
  6.1 3.3 %collective-permute-start.7 = (bf16[32,8]{0,1:T(8,128)(2,1)S(1)}, bf16[32,8]{0,1:T(8,128)(2,1)S(1)}, u32[]{:S(2)}, u32[]{:S(2)}) collective-permute-start(bf16[32,8]{0,1:T(8,128)(2,1)S(1)} %get-tuple-element.6), channel_id=1, source_target_pairs={{16,0},{24,8},{32,16},{40,24},{48,32},{56,40},{64,48},{72,56},{80,... | collective-permute-start | bytes 1544 | tf_op jit(solution)/shard_map/ppermute | solution.py:33
  9.4 3.1 %collective-permute-start.8 = (bf16[32,8]{0,1:T(8,128)(2,1)S(1)}, bf16[32,8]{0,1:T(8,128)(2,1)S(1)}, u32[]{:S(2)}, u32[]{:S(2)}) collective-permute-start(bf16[32,8]{0,1:T(8,128)(2,1)S(1)} %get-tuple-element.6), channel_id=1, source_target_pairs={{24,0},{32,8},{40,16},{48,24},{56,32},{64,40},{72,48},{80,56},{88,... | collective-permute-start | bytes 1544 | tf_op jit(solution)/shard_map/ppermute | solution.py:33
  12.5 3.1 %collective-permute-start.9 = (bf16[32,8]{0,1:T(8,128)(2,1)S(1)}, bf16[32,8]{0,1:T(8,128)(2,1)S(1)}, u32[]{:S(2)}, u32[]{:S(2)}) collective-permute-start(bf16[32,8]{0,1:T(8,128)(2,1)S(1)} %get-tuple-element.6), channel_id=1, source_target_pairs={{32,0},{40,8},{48,16},{56,24},{64,32},{72,40},{80,48},{88,56},{96,... | collective-permute-start | bytes 1544 | tf_op jit(solution)/shard_map/ppermute | solution.py:33
  15.6 1.4 abs.9
  17.1 0.3 copy.44
  17.4 0.5 fusion.57
  17.8 2.5 multiply_add_fusion
  20.4 1.8 add.81
  22.2 1.2 multiply_convert_fusion.2
  23.5 0.4 convolution_bitcast_fusion
  24.0 3.4 %collective-permute-start = (bf16[32,256]{0,1:T(8,128)(2,1)S(1)}, bf16[32,256]{0,1:T(8,128)(2,1)S(1)}, u32[]{:S(2)}, u32[]{:S(2)}) collective-permute-start(bf16[32,256]{0,1:T(8,128)(2,1)S(1)} %fusion.39), channel_id=1, source_target_pairs={{0,1},{1,2},{2,3},{3,4},{4,5},{5,6},{6,7},{8,9},{9,10},{10,11},{11... | collective-permute-start | bytes 49160 | tf_op jit(solution)/shard_map/ppermute | solution.py:22
  27.5 1.3 collective-permute-start.1
  29.4 4.2 %collective-permute-done.1 = bf16[32,256]{0,1:T(8,128)(2,1)S(1)} collective-permute-done((bf16[32,256]{0,1:T(8,128)(2,1)S(1)}, bf16[32,256]{0,1:T(8,128)(2,1)S(1)}, u32[]{:S(2)}, u32[]{:S(2)}) %collective-permute-start.1) | collective-permute-done | bytes 16416 | tf_op jit(solution)/shard_map/ppermute | solution.py:25
  34.1 1.9 collective-permute-start.2
  36.0 2.4 collective-permute-start.3
  38.4 2.1 collective-permute-start.4
  40.4 4.3 %collective-permute-start.5 = (bf16[32,512]{0,1:T(8,128)(2,1)S(1)}, bf16[32,512]{0,1:T(8,128)(2,1)S(1)}, u32[]{:S(2)}, u32[]{:S(2)}) collective-permute-start(bf16[32,512]{0,1:T(8,128)(2,1)S(1)} %bitcast.68), channel_id=1, source_target_pairs={{32,0},{40,8},{48,16},{56,24},{64,32},{72,40},{80,48},{88,56},{96,... | collective-permute-start | bytes 98312 | tf_op jit(solution)/shard_map/ppermute | solution.py:33
  45.7 8.3 %collective-permute-done.4 = bf16[32,512]{0,1:T(8,128)(2,1)S(1)} collective-permute-done((bf16[32,512]{0,1:T(8,128)(2,1)S(1)}, bf16[32,512]{0,1:T(8,128)(2,1)S(1)}, u32[]{:S(2)}, u32[]{:S(2)}) %collective-permute-start.4) | collective-permute-done | bytes 32800 | tf_op jit(solution)/shard_map/ppermute | solution.py:33
  54.2 2.1 collective-permute-done.5
  56.6 0.3 concatenate.55
  56.9 0.4 fusion.29
  57.3 0.6 reshape.192
  58.2 1.4 reshape.193
  60.5 0.3 concatenate.49
  60.7 0.4 fusion.58
  61.1 0.6 reshape.187
  62.0 2.4 reshape.188
  64.5 1.1 fusion.33
  65.7 2.5 collective-permute-start.10
  68.2 1.9 collective-permute-start.11
  70.1 2.2 collective-permute-start.12
  72.4 2.7 collective-permute-start.13
  75.1 28.0 %collective-permute-done.10 = bf16[2,32,32,128]{3,2,1,0:T(8,128)(2,1)S(1)} collective-permute-done((bf16[2,32,32,128]{3,2,1,0:T(8,128)(2,1)S(1)}, bf16[2,32,32,128]{3,2,1,0:T(8,128)(2,1)S(1)}, u32[]{:S(2)}, u32[]{:S(2)}) %collective-permute-start.10) | collective-permute-done | bytes 524320 | tf_op jit(solution)/shard_map/ppermute | solution.py:33
  103.1 13.2 %collective-permute-done.11 = bf16[2,32,32,128]{3,2,1,0:T(8,128)(2,1)S(1)} collective-permute-done((bf16[2,32,32,128]{3,2,1,0:T(8,128)(2,1)S(1)}, bf16[2,32,32,128]{3,2,1,0:T(8,128)(2,1)S(1)}, u32[]{:S(2)}, u32[]{:S(2)}) %collective-permute-start.11) | collective-permute-done | bytes 524320 | tf_op jit(solution)/shard_map/ppermute | solution.py:33
  116.4 37.7 %collective-permute-done.12 = bf16[2,32,32,128]{3,2,1,0:T(8,128)(2,1)S(1)} collective-permute-done((bf16[2,32,32,128]{3,2,1,0:T(8,128)(2,1)S(1)}, bf16[2,32,32,128]{3,2,1,0:T(8,128)(2,1)S(1)}, u32[]{:S(2)}, u32[]{:S(2)}) %collective-permute-start.12) | collective-permute-done | bytes 524320 | tf_op jit(solution)/shard_map/ppermute | solution.py:33
  154.2 4.4 %collective-permute-done.13 = bf16[2,32,32,128]{3,2,1,0:T(8,128)(2,1)S(1)} collective-permute-done((bf16[2,32,32,128]{3,2,1,0:T(8,128)(2,1)S(1)}, bf16[2,32,32,128]{3,2,1,0:T(8,128)(2,1)S(1)}, u32[]{:S(2)}, u32[]{:S(2)}) %collective-permute-start.13) | collective-permute-done | bytes 524320 | tf_op jit(solution)/shard_map/ppermute | solution.py:33
  158.8 1.5 copy-done
  160.3 55.1 %rev.13 = bf16[2,32,128,160]{2,3,1,0:T(8,128)(2,1)S(1)} reverse(bf16[2,32,128,160]{2,3,1,0:T(8,128)(2,1)} %bitcast.54), dimensions={2} | reverse | bytes 5242880 | tf_op jit(solution)/shard_map/jit(_flip)/rev | solution.py:152
  215.4 4.2 %copy.38 = bf16[2,32,128,160]{3,2,1,0:T(8,128)(2,1)} copy(bf16[2,32,128,160]{2,3,1,0:T(8,128)(2,1)S(1)} %rev.13) | data formatting | bytes 5242880 | tf_op jit(solution)/shard_map/jit(_flip)/rev | solution.py:152
  219.6 9.5 %reshape.194 = bf16[2,32,20480]{2,1,0:T(8,128)(2,1)} reshape(bf16[2,32,128,160]{3,2,1,0:T(8,128)(2,1)} %copy.38) | data formatting | bytes 5242880 | tf_op jit(solution)/shard_map/reshape | solution.py:40
  229.1 1.9 pad.20
  231.0 12.8 %reshape.195 = bf16[2,32,128,161]{3,2,1,0:T(8,128)(2,1)} reshape(bf16[2,32,20608]{2,1,0:T(8,128)(2,1)S(1)} %pad.20) | data formatting | bytes 5275648 | tf_op jit(solution)/shard_map/reshape | solution.py:43
  243.8 1.6 slice-done
  245.4 20.1 %rev.14 = bf16[2,32,128,32]{3,2,1,0:T(8,128)(2,1)} reverse(bf16[2,32,128,32]{3,2,1,0:T(8,128)(2,1)S(1)} %slice-done), dimensions={2} | reverse | bytes 1048576 | tf_op jit(solution)/shard_map/jit(_flip)/rev | solution.py:153
  265.5 1.8 multiply_bitcast_fusion
  267.3 1.5 copy.39
  (54 shorter events, 4.2 us)
Async XLA Ops:
  1.3 26.2 %collective-permute-start.6 = (bf16[32,8]{0,1:T(8,128)(2,1)S(1)}, bf16[32,8]{0,1:T(8,128)(2,1)S(1)}, u32[]{:S(2)}, u32[]{:S(2)}) collective-permute-start(bf16[32,8]{0,1:T(8,128)(2,1)S(1)} %get-tuple-element.6), channel_id=1, source_target_pairs={{8,0},{16,8},{24,16},{32,24},{40,32},{48,40},{56,48},{64,56},{72,6... | collective-permute-start | bytes 1544 | tf_op jit(solution)/shard_map/ppermute | solution.py:33
  6.1 22.7 %collective-permute-start.7 = (bf16[32,8]{0,1:T(8,128)(2,1)S(1)}, bf16[32,8]{0,1:T(8,128)(2,1)S(1)}, u32[]{:S(2)}, u32[]{:S(2)}) collective-permute-start(bf16[32,8]{0,1:T(8,128)(2,1)S(1)} %get-tuple-element.6), channel_id=1, source_target_pairs={{16,0},{24,8},{32,16},{40,24},{48,32},{56,40},{64,48},{72,56},{80,... | collective-permute-start | bytes 1544 | tf_op jit(solution)/shard_map/ppermute | solution.py:33
  9.4 19.4 %collective-permute-start.8 = (bf16[32,8]{0,1:T(8,128)(2,1)S(1)}, bf16[32,8]{0,1:T(8,128)(2,1)S(1)}, u32[]{:S(2)}, u32[]{:S(2)}) collective-permute-start(bf16[32,8]{0,1:T(8,128)(2,1)S(1)} %get-tuple-element.6), channel_id=1, source_target_pairs={{24,0},{32,8},{40,16},{48,24},{56,32},{64,40},{72,48},{80,56},{88,... | collective-permute-start | bytes 1544 | tf_op jit(solution)/shard_map/ppermute | solution.py:33
  12.5 16.3 %collective-permute-start.9 = (bf16[32,8]{0,1:T(8,128)(2,1)S(1)}, bf16[32,8]{0,1:T(8,128)(2,1)S(1)}, u32[]{:S(2)}, u32[]{:S(2)}) collective-permute-start(bf16[32,8]{0,1:T(8,128)(2,1)S(1)} %get-tuple-element.6), channel_id=1, source_target_pairs={{32,0},{40,8},{48,16},{56,24},{64,32},{72,40},{80,48},{88,56},{96,... | collective-permute-start | bytes 1544 | tf_op jit(solution)/shard_map/ppermute | solution.py:33
  20.4 3.1 %copy-start.1 = (bf16[32,8,2048]{2,1,0:T(8,128)(2,1)S(1)}, bf16[32,8,2048]{2,1,0:T(8,128)(2,1)}, u32[]{:S(2)}) copy-start(bf16[32,8,2048]{2,1,0:T(8,128)(2,1)} %param.4) | copy-start | bytes 3145732
  23.9 32.9 %copy-start.4 = (bf16[16]{0:T(256)(128)(2,1)S(1)}, bf16[16]{0:T(256)(128)(2,1)}, u32[]{:S(2)}) copy-start(bf16[16]{0:T(256)(128)(2,1)} %constant.56.clone.1) | copy-start | bytes 100
  24.0 5.4 %collective-permute-start = (bf16[32,256]{0,1:T(8,128)(2,1)S(1)}, bf16[32,256]{0,1:T(8,128)(2,1)S(1)}, u32[]{:S(2)}, u32[]{:S(2)}) collective-permute-start(bf16[32,256]{0,1:T(8,128)(2,1)S(1)} %fusion.39), channel_id=1, source_target_pairs={{0,1},{1,2},{2,3},{3,4},{4,5},{5,6},{6,7},{8,9},{9,10},{10,11},{11... | collective-permute-start | bytes 49160 | tf_op jit(solution)/shard_map/ppermute | solution.py:22
  27.5 6.1 %collective-permute-start.1 = (bf16[32,256]{0,1:T(8,128)(2,1)S(1)}, bf16[32,256]{0,1:T(8,128)(2,1)S(1)}, u32[]{:S(2)}, u32[]{:S(2)}) collective-permute-start(bf16[32,256]{0,1:T(8,128)(2,1)S(1)} %fusion.39), channel_id=1, source_target_pairs={{1,0},{2,1},{3,2},{4,3},{5,4},{6,5},{7,6},{9,8},{10,9},{11,10},{12... | collective-permute-start | bytes 49160 | tf_op jit(solution)/shard_map/ppermute | solution.py:25
  34.1 11.2 %collective-permute-start.2 = (bf16[32,512]{0,1:T(8,128)(2,1)S(1)}, bf16[32,512]{0,1:T(8,128)(2,1)S(1)}, u32[]{:S(2)}, u32[]{:S(2)}) collective-permute-start(bf16[32,512]{0,1:T(8,128)(2,1)S(1)} %bitcast.65), channel_id=1, source_target_pairs={{8,0},{16,8},{24,16},{32,24},{40,32},{48,40},{56,48},{64,56},{72,6... | collective-permute-start | bytes 98312 | tf_op jit(solution)/shard_map/ppermute | solution.py:33
  36.0 9.5 %collective-permute-start.3 = (bf16[32,512]{0,1:T(8,128)(2,1)S(1)}, bf16[32,512]{0,1:T(8,128)(2,1)S(1)}, u32[]{:S(2)}, u32[]{:S(2)}) collective-permute-start(bf16[32,512]{0,1:T(8,128)(2,1)S(1)} %bitcast.66), channel_id=1, source_target_pairs={{16,0},{24,8},{32,16},{40,24},{48,32},{56,40},{64,48},{72,56},{80,... | collective-permute-start | bytes 98312 | tf_op jit(solution)/shard_map/ppermute | solution.py:33
  38.4 15.7 %collective-permute-start.4 = (bf16[32,512]{0,1:T(8,128)(2,1)S(1)}, bf16[32,512]{0,1:T(8,128)(2,1)S(1)}, u32[]{:S(2)}, u32[]{:S(2)}) collective-permute-start(bf16[32,512]{0,1:T(8,128)(2,1)S(1)} %bitcast.67), channel_id=1, source_target_pairs={{24,0},{32,8},{40,16},{48,24},{56,32},{64,40},{72,48},{80,56},{88,... | collective-permute-start | bytes 98312 | tf_op jit(solution)/shard_map/ppermute | solution.py:33
  40.4 15.9 %collective-permute-start.5 = (bf16[32,512]{0,1:T(8,128)(2,1)S(1)}, bf16[32,512]{0,1:T(8,128)(2,1)S(1)}, u32[]{:S(2)}, u32[]{:S(2)}) collective-permute-start(bf16[32,512]{0,1:T(8,128)(2,1)S(1)} %bitcast.68), channel_id=1, source_target_pairs={{32,0},{40,8},{48,16},{56,24},{64,32},{72,40},{80,48},{88,56},{96,... | collective-permute-start | bytes 98312 | tf_op jit(solution)/shard_map/ppermute | solution.py:33
  65.7 93.1 %copy-start.2 = (bf16[2,32,32,128]{3,2,1,0:T(8,128)(2,1)}, bf16[2,32,32,128]{3,2,1,0:T(8,128)(2,1)S(1)}, u32[]{:S(2)}) copy-start(bf16[2,32,32,128]{3,2,1,0:T(8,128)(2,1)S(1)} %pad_maximum_fusion) | copy-start | bytes 1572868
  65.7 37.4 %collective-permute-start.10 = (bf16[2,32,32,128]{3,2,1,0:T(8,128)(2,1)S(1)}, bf16[2,32,32,128]{3,2,1,0:T(8,128)(2,1)S(1)}, u32[]{:S(2)}, u32[]{:S(2)}) collective-permute-start(bf16[2,32,32,128]{3,2,1,0:T(8,128)(2,1)S(1)} %pad_maximum_fusion), channel_id=1, source_target_pairs={{0,32},{8,40},{16,48},{24,56},{32,64},{40,72},{48,80},{56,88},{64,... | collective-permute-start | bytes 1572872 | tf_op jit(solution)/shard_map/ppermute | solution.py:33
  68.2 48.1 %collective-permute-start.11 = (bf16[2,32,32,128]{3,2,1,0:T(8,128)(2,1)S(1)}, bf16[2,32,32,128]{3,2,1,0:T(8,128)(2,1)S(1)}, u32[]{:S(2)}, u32[]{:S(2)}) collective-permute-start(bf16[2,32,32,128]{3,2,1,0:T(8,128)(2,1)S(1)} %pad_maximum_fusion), channel_id=1, source_target_pairs={{0,24},{8,32},{16,40},{24,48},{32,56},{40,64},{48,72},{56,80},{64,... | collective-permute-start | bytes 1572872 | tf_op jit(solution)/shard_map/ppermute | solution.py:33
  70.1 84.0 %collective-permute-start.12 = (bf16[2,32,32,128]{3,2,1,0:T(8,128)(2,1)S(1)}, bf16[2,32,32,128]{3,2,1,0:T(8,128)(2,1)S(1)}, u32[]{:S(2)}, u32[]{:S(2)}) collective-permute-start(bf16[2,32,32,128]{3,2,1,0:T(8,128)(2,1)S(1)} %pad_maximum_fusion), channel_id=1, source_target_pairs={{0,16},{8,24},{16,32},{24,40},{32,48},{40,56},{48,64},{56,72},{64,... | collective-permute-start | bytes 1572872 | tf_op jit(solution)/shard_map/ppermute | solution.py:33
  72.4 86.2 %collective-permute-start.13 = (bf16[2,32,32,128]{3,2,1,0:T(8,128)(2,1)S(1)}, bf16[2,32,32,128]{3,2,1,0:T(8,128)(2,1)S(1)}, u32[]{:S(2)}, u32[]{:S(2)}) collective-permute-start(bf16[2,32,32,128]{3,2,1,0:T(8,128)(2,1)S(1)} %pad_maximum_fusion), channel_id=1, source_target_pairs={{0,8},{8,16},{16,24},{24,32},{32,40},{40,48},{48,56},{56,64},{64,7... | collective-permute-start | bytes 1572872 | tf_op jit(solution)/shard_map/ppermute | solution.py:33
  158.7 1.5 copy-start
  243.8 1.6 slice-start
  245.4 20.1 %copy-start.3 = (bf16[2]{0:T(256)(128)(2,1)S(1)}, bf16[2]{0:T(256)(128)(2,1)}, u32[]{:S(2)}) copy-start(bf16[2]{0:T(256)(128)(2,1)} %constant.57.clone) | copy-start | bytes 16
where the time goes:
time: 274 us; the launch traced here: 269 us
  local copies, waits for them, and re-layouts  120 us (44%)
  waiting for transfers between devices  98 us (36%)
  starting transfers between devices  39 us (14%)
  other arithmetic  6.66 us (2%)
  matrix products  4.19 us (2%)
    ppermute x12, waiting for transfers between devices, from_behind(): return lax.ppermute(value, axis, pairs)  93.8 us
    rev x2, local copies, waits for them, and re-layouts, per_device(): turned = jnp.flip(jnp.swapaxes(joined, 2, 3), axis=2)  59.3 us
    ppermute x12, starting transfers between devices, from_behind(): return lax.ppermute(value, axis, pairs)  34.3 us
    rev x1, local copies, waits for them, and re-layouts, per_device(): picked = jnp.flip(skew_take(turned, behind_offset, channels), axis=2)  20.1 us
    reshape x4, local copies, waits for them, and re-layouts, skew_take(): flattened.reshape(leading + (row_count, col_count + 1))[..., :reach_cols]  16.8 us
    reshape x4, local copies, waits for them, and re-layouts, skew_take(): dense_mat.reshape(leading + (row_count * col_count,))[..., offset:]  10.8 us
  transfers between devices with their start and end apart: 14, of which 7 were waited for; matrix products, arithmetic and copies ran while one was open for 4% of the time, Pallas kernels for 0%

commit v1 on v0

v1 whole, which is shorter than its diff:
```python
import functools
import math

import jax
import jax.numpy as jnp
from jax import lax
from jax.experimental import pallas as pl
from jax.experimental.pallas import tpu as pltpu
from jax.sharding import PartitionSpec as P

WINDOWS = 8
SAMPLES = 2048
REACH = 128
TIME_HALF = 128
BIN_HALF = 32
LOCAL = 32
AHEAD = REACH // LOCAL
BLOCK = 256
ROWS = LOCAL * WINDOWS
GROUPS = 2
CHUNKS = 2
STEPS = 4
F32 = jnp.float32
BF16 = jnp.bfloat16
MESH = pl.DeviceIdType.MESH

SLOT_AHEAD = (0, 1, 2, 3, 8)
SLOT_BEHIND = (5, 6, 7, 4, 9)
SLOTS = 12


def iota(shape, axis):
    return lax.broadcasted_iota(jnp.int32, shape, axis)


def cos_sin(index):
    quarter = SAMPLES // 4
    turn = (index + quarter // 2) // quarter
    x = (index - turn * quarter).astype(F32) * (2.0 * math.pi / SAMPLES)
    y = x * x
    s = x * (1.0 + y * (-1 / 6 + y * (1 / 120 + y * (-1 / 5040 + y * (1 / 362880)))))
    c = 1.0 + y * (-1 / 2 + y * (1 / 24 + y * (-1 / 720 + y * (1 / 40320))))
    turn = turn & 3
    odd = (turn & 1) == 1
    cos = jnp.where(odd, s, c)
    sin = jnp.where(odd, c, s)
    cos = jnp.where((turn == 1) | (turn == 2), -cos, cos)
    sin = jnp.where(turn >= 2, -sin, sin)
    return cos, sin


def lane_bin(lane):
    block = lane // 64
    within = (lane // 32) % 2 * 16 + lane % 16
    return within + jnp.where(block == 1, -LOCAL, jnp.where(block == 2, LOCAL, 0))


def front_kernel(
    ahead_count, bins, strain_ref, ok_ref, window_ref, gath_ref, use_ref,
    x_ref, table_ref, base_ref, ring_ref, spread_ref, band_ref, white_ref,
    in_sem, use_send, use_recv, send_sem, recv_sem,
):
    me = lax.axis_index("ch")
    first_bin = lax.axis_index("freq") * LOCAL + 1
    rows = ROWS // CHUNKS
    channels = LOCAL // CHUNKS

    loads = []
    for chunk in range(CHUNKS):
        part = pl.ds(chunk * rows, rows)
        loads.append(pltpu.make_async_copy(strain_ref.at[part], x_ref.at[part], in_sem.at[chunk]))
        loads[-1].start()

    barrier = pltpu.get_barrier_semaphore()
    peers = jnp.int32(0)
    for distance in range(1, AHEAD + 1):
        for step in (distance, -distance):
            there = (me + step >= 0) & (me + step < ahead_count)
            peers = peers + there.astype(jnp.int32)

            @pl.when(there)
            def _():
                pl.semaphore_signal(barrier, 1, device_id={"ch": me + step}, device_id_type=MESH)

    diagonal = iota((LOCAL, LOCAL), 0) == iota((LOCAL, LOCAL), 1)
    healthy = jnp.sum(jnp.where(diagonal, ok_ref[...].astype(F32), 0.0), axis=1, keepdims=True)
    usable8 = (window_ref[...].astype(F32) * healthy).astype(BF16)
    widen = (iota((WINDOWS, 128), 0) == iota((WINDOWS, 128), 1)).astype(BF16)
    usable = jnp.dot(usable8, widen, preferred_element_type=F32).astype(BF16)
    flip = (iota((LOCAL, LOCAL), 0) + iota((LOCAL, LOCAL), 1) == LOCAL - 1).astype(BF16)
    use_ref[SLOT_AHEAD[0]] = usable
    use_ref[SLOT_BEHIND[0]] = jnp.dot(flip, usable, preferred_element_type=F32).astype(BF16)
    keep = []
    for half in range(2):
        expand = (iota((128, 128), 0) == 4 * half + iota((128, 128), 1) // 32).astype(BF16)
        keep.append(jnp.dot(usable, expand, preferred_element_type=F32))

    for slot in range(10, SLOTS):
        gath_ref[slot] = jnp.zeros((LOCAL, 512), BF16)
        use_ref[slot] = jnp.zeros((LOCAL, 128), BF16)
    for distance in range(1, AHEAD + 1):
        for step, slot in ((distance, SLOT_AHEAD[distance]), (-distance, SLOT_BEHIND[distance])):
            absent = (me + step < 0) | (me + step >= ahead_count)

            @pl.when(absent)
            def _():
                gath_ref[slot] = jnp.zeros((LOCAL, 512), BF16)
                use_ref[slot] = jnp.zeros((LOCAL, 128), BF16)

    distance_in = iota((2 * BLOCK, BLOCK), 0) - TIME_HALF - iota((2 * BLOCK, BLOCK), 1)
    spread_ref[...] = (jnp.abs(distance_in) <= TIME_HALF).astype(BF16)

    source = iota((BLOCK, 128), 0)
    target = iota((BLOCK, 128), 1)
    source_bin = lane_bin(source) + first_bin
    near = jnp.abs(source_bin - (lane_bin(target) + first_bin)) <= BIN_HALF
    inside = (source_bin >= 1) & (source_bin <= bins) & (source < 192) & (target < 64)
    band_ref[...] = (near & inside).astype(BF16)

    row = iota((48, BLOCK), 0)
    step_of = jnp.where(row < 32, 8 * row, jnp.where(row < 40, row - 32, 256 * (row - 40)))
    lane = iota((48, BLOCK), 1)
    cos, sin = cos_sin(((lane_bin(lane) + first_bin) * step_of) & (SAMPLES - 1))
    imaginary = (iota((8, BLOCK), 1) // 16) % 2 == 1
    cos1, sin1 = cos[32:40], sin[32:40]
    for i in range(32):
        c8, s8 = cos[i : i + 1], sin[i : i + 1]
        c = c8 * cos1 - s8 * sin1
        s = s8 * cos1 + c8 * sin1
        base_ref[0, pl.ds(8 * i, 8)] = jnp.where(imaginary, -s, c)
        base_ref[1, pl.ds(8 * i, 8)] = jnp.where(imaginary, -c, -s)
    scale = 1.0 / math.sqrt(SAMPLES)
    ring_ref[0] = cos[40:48] * scale
    ring_ref[1] = sin[40:48] * scale
    for c in range(SAMPLES // BLOCK):
        table_ref[pl.ds(c * BLOCK, BLOCK)] = (
            base_ref[0] * ring_ref[0, pl.ds(c, 1)] + base_ref[1] * ring_ref[1, pl.ds(c, 1)]
        ).astype(BF16)

    pl.semaphore_wait(barrier, peers)

    def copies(step, part):
        own, slot = (SLOT_BEHIND[0], SLOT_BEHIND[step]) if step > 0 else (SLOT_AHEAD[0], SLOT_AHEAD[-step])
        which = (step + AHEAD) if step < 0 else (step + AHEAD - 1)
        if part is None:
            src, dst, send, recv = use_ref.at[own], use_ref.at[slot], use_send.at[which], use_recv.at[which]
        else:
            at = pl.ds((CHUNKS - 1 - part if step > 0 else part) * channels, channels)
            src, dst = gath_ref.at[own, at], gath_ref.at[slot, at]
            send, recv = send_sem.at[part, which], recv_sem.at[part, which]
        return pltpu.make_async_remote_copy(
            src_ref=src, dst_ref=dst, send_sem=send, recv_sem=recv, device_id={"ch": me + step}, device_id_type=MESH
        )

    steps = [s * d for d in range(AHEAD, 0, -1) for s in (1, -1)]

    def for_each(part, act):
        for step in steps:
            @pl.when((me + step >= 0) & (me + step < ahead_count))
            def _():
                act(copies(step, part))

    def for_each_source(part, act):
        for step in steps:
            @pl.when((me - step >= 0) & (me - step < ahead_count))
            def _():
                act(copies(step, part))

    for_each(None, lambda copy: copy.start())

    lanes = iota((channels, 128), 1) // 32
    flip = (iota((channels, channels), 0) + iota((channels, channels), 1) == channels - 1).astype(BF16)
    for chunk in range(CHUNKS):
        loads[chunk].wait()
        part = pl.ds(chunk * rows, rows)
        spectrum = jnp.zeros((rows, BLOCK), F32)
        for block in range(SAMPLES // BLOCK):
            low = max(block * BLOCK - TIME_HALF, 0)
            high = min(block * BLOCK + BLOCK + TIME_HALF, SAMPLES)
            skip = low - (block * BLOCK - TIME_HALF)
            sums = jnp.dot(
                jnp.abs(x_ref[part, low:high]), spread_ref[skip : skip + high - low], preferred_element_type=F32
            )
            level = sums * (1.0 / (2 * TIME_HALF + 1)) + 1e-06
            leveled = (x_ref[part, block * BLOCK : (block + 1) * BLOCK].astype(F32) / level).astype(BF16)
            spectrum = spectrum + jnp.dot(
                leveled, table_ref[block * BLOCK : (block + 1) * BLOCK], preferred_element_type=F32
            )
        power = spectrum * spectrum
        coarse = power.astype(BF16)
        fine = (power - coarse.astype(F32)).astype(BF16)
        smooth = jnp.dot(coarse, band_ref[...], preferred_element_type=F32) + jnp.dot(
            fine, band_ref[...], preferred_element_type=F32
        )
        white_ref[part] = spectrum[:, :128] * lax.rsqrt(smooth * (1.0 / (2 * BIN_HALF + 1)) + 1e-06)
        at = chunk * channels
        by_window = [white_ref[pl.ds(chunk * rows + w, channels, stride=WINDOWS)] for w in range(WINDOWS)]
        for group in range(GROUPS):
            for half in range(2):
                piece = None
                for i in range(4):
                    moved = pltpu.roll(by_window[4 * half + i], (32 * (i - group)) % 128, 1)
                    piece = moved if piece is None else jnp.where(lanes == i, moved, piece)
                piece = (piece * keep[half][at : at + channels]).astype(BF16)
                where = pl.ds((2 * group + half) * 128, 128)
                gath_ref[SLOT_AHEAD[0], pl.ds(at, channels), where] = piece
                gath_ref[SLOT_BEHIND[0], pl.ds(LOCAL - at - channels, channels), where] = jnp.dot(
                    flip, piece, preferred_element_type=F32
                ).astype(BF16)
        for_each(chunk, lambda copy: copy.start())

    for part in (None, *range(CHUNKS)):
        for_each_source(part, lambda copy: copy.wait_recv())
        for_each(part, lambda copy: copy.wait_send())


def front(strain, channel_ok, window_ok, ahead_count, bins):
    return pl.pallas_call(
        functools.partial(front_kernel, ahead_count, bins),
        out_shape=(
            jax.ShapeDtypeStruct((SLOTS, LOCAL, 512), BF16),
            jax.ShapeDtypeStruct((SLOTS, LOCAL, 128), BF16),
        ),
        in_specs=[
            pl.BlockSpec(memory_space=pl.ANY),
            pl.BlockSpec(memory_space=pltpu.VMEM),
            pl.BlockSpec(memory_space=pltpu.VMEM),
        ],
        out_specs=(pl.BlockSpec(memory_space=pltpu.VMEM), pl.BlockSpec(memory_space=pltpu.VMEM)),
        scratch_shapes=[
            pltpu.VMEM((ROWS, SAMPLES), BF16),
            pltpu.VMEM((SAMPLES, BLOCK), BF16),
            pltpu.VMEM((2, BLOCK, BLOCK), F32),
            pltpu.VMEM((2, 8, BLOCK), F32),
            pltpu.VMEM((2 * BLOCK, BLOCK), BF16),
            pltpu.VMEM((BLOCK, 128), BF16),
            pltpu.VMEM((ROWS, 128), F32),
            pltpu.SemaphoreType.DMA((CHUNKS,)),
            pltpu.SemaphoreType.DMA((2 * AHEAD,)),
            pltpu.SemaphoreType.DMA((2 * AHEAD,)),
            pltpu.SemaphoreType.DMA((CHUNKS, 2 * AHEAD)),
            pltpu.SemaphoreType.DMA((CHUNKS, 2 * AHEAD)),
        ],
        compiler_params=pltpu.CompilerParams(collective_id=0, has_side_effects=True),
        name="front",
    )(strain.reshape(ROWS, SAMPLES), channel_ok.reshape(1, LOCAL), window_ok)


def lag_rows(ahead, behind, tail):
    row = iota((LOCAL, 128), 0)
    lane = iota((LOCAL, 128), 1)
    ahead = jnp.where(lane <= row, tail, ahead)
    behind = jnp.where((lane >= 32) & (lane < 64 - row), tail, behind)
    return (
        jnp.take_along_axis(ahead, (lane + row + 1) & 127, axis=1),
        pltpu.roll(behind, 64, 1, stride=1, stride_axis=0),
    )


def cross_kernel(gath_ref, use_ref, ahead_ref, behind_ref, scale_ref, lhs_ref):
    step = pl.program_id(0)
    per_step = LOCAL // STEPS

    @pl.when(step == 0)
    def _():
        pairs = lax.dot_general(
            use_ref[0], use_ref[...].reshape(SLOTS * LOCAL, 128), (((1,), (1,)), ((), ())), preferred_element_type=F32
        )
        for side, count in enumerate(lag_rows(pairs[:, :128], pairs[:, 128:256], pairs[:, 256:])):
            scale_ref[side] = 1.0 / jnp.maximum(count, 1.0)

    at = pl.ds(pl.multiple_of(step // (STEPS // GROUPS) * 256, 256), 256)
    own = gath_ref[0, :, at]
    wide = own.astype(F32)
    swap = jnp.where((iota((LOCAL, 256), 1) // 16) % 2 == 0, -pltpu.roll(wide, 240, 1), pltpu.roll(wide, 16, 1)).astype(BF16)
    lane_of = iota((LOCAL, 256), 1) % 16
    first = step % (STEPS // GROUPS) * per_step
    for part, value in enumerate((own, swap)):
        for f in range(per_step):
            lhs_ref[pl.ds((part * per_step + f) * LOCAL, LOCAL)] = jnp.where(
                lane_of == first + f, value, jnp.zeros_like(value)
            )
    rhs = gath_ref[:, :, at].reshape(SLOTS * LOCAL, 256)
    cross = lax.dot_general(lhs_ref[...], rhs, (((1,), (1,)), ((), ())), preferred_element_type=F32)
    for part in range(2):
        for f in range(per_step):
            rows = slice((part * per_step + f) * LOCAL, (part * per_step + f + 1) * LOCAL)
            ahead, behind = lag_rows(cross[rows, :128], cross[rows, 128:256], cross[rows, 256:])
            ahead_ref[part, f] = (ahead * scale_ref[0]).astype(BF16)
            behind_ref[part, f] = (behind * scale_ref[1]).astype(BF16)


def cross(gathered, usable):
    per_step = LOCAL // STEPS
    out = jax.ShapeDtypeStruct((2, LOCAL, LOCAL, REACH), BF16)
    out_spec = pl.BlockSpec((2, per_step, LOCAL, REACH), lambda i: (0, i, 0, 0))
    return pl.pallas_call(
        cross_kernel,
        grid=(STEPS,),
        out_shape=(out, out),
        in_specs=[pl.BlockSpec(memory_space=pltpu.VMEM), pl.BlockSpec(memory_space=pltpu.VMEM)],
        out_specs=(out_spec, out_spec),
        scratch_shapes=[
            pltpu.VMEM((2, LOCAL, 128), F32),
            pltpu.VMEM((2 * per_step * LOCAL, 256), BF16),
        ],
        name="cross",
    )(gathered, usable)


def solution(mesh):
    ahead_count = mesh.shape["ch"]
    bins = LOCAL * mesh.shape["freq"]

    def per_device(strain, channel_ok, window_ok):
        gathered, usable = front(strain, channel_ok, window_ok, ahead_count, bins)
        return cross(gathered, usable)

    return jax.shard_map(
        per_device,
        mesh=mesh,
        in_specs=(P("ch", None, None), P("ch"), P("ch", None)),
        out_specs=(P(None, "freq", "ch", None), P(None, "freq", "ch", None)),
        check_vma=False,
    )
```

time: 274 us -> 23.6 us (0.09)
  the two profiles are of different devices: /device:TPU:384 before, /device:TPU:256 now
where the time goes in v1:
time: 23.6 us; the launch traced here: 23.3 us
  Pallas kernels  21.3 us (90%)
  local copies, waits for them, and re-layouts  1.37 us (6%)
  between operations  0.64 us (3%)
    pallas_call x1, Pallas kernels, front(): pl.pallas_call(functools.partial(front_kernel, ahead_count, bins), out_sh...  17.1 us
    pallas_call x1, Pallas kernels, cross(): pl.pallas_call(cross_kernel, grid=(STEPS,), out_shape=(out, out), in_spec...  4.24 us
    unnamed x1, local copies, waits for them, and re-layouts  1.37 us

profile of v1, /device:TPU:256, one launch (start us, length us, event | category | flops | bytes accessed | tf_op | source)
XLA Modules:
  0.0 23.3 jit_solution(10331610728687633511)
XLA Ops:
  0.6 1.4 %copy.5.window_ref = s32[32,8]{1,0:T(8,128)} copy(s32[32,8]{0,1:T(8,128)} %param.5) | data formatting | bytes 2048 | tf_op args[2]
  2.0 17.1 %front.1 = (bf16[12,32,512]{2,1,0:T(8,128)(2,1)}, bf16[12,32,128]{2,1,0:T(8,128)(2,1)}) custom-call(bf16[256,2048]{1,0:T(8,128)(2,1)} %bitcast.2, s32[1,32]{1,0:T(1,128)} %bitcast.3, s32[32,8]{1,0:T(8,128)} %copy.5.window_ref), custom_call_target="tpu_custom_call" | custom-call | tf_op jit(solution)/shard_map/front/pallas_call | solution.py:218
  19.1 4.2 %cross.1 = (bf16[2,32,32,128]{3,2,1,0:T(8,128)(2,1)}, bf16[2,32,32,128]{3,2,1,0:T(8,128)(2,1)}) custom-call(bf16[12,32,512]{2,1,0:T(8,128)(2,1)} %get-tuple-element.4.gath_ref, bf16[12,32,128]{2,1,0:T(8,128)(2,1)} %get-tuple-element.5.use_ref), custom_call_target="tpu_custom_call" | custom-call | tf_op jit(solution)/shard_map/cross/pallas_call | solution.py:297

commit v2 on v1

v2 whole, which is shorter than its diff:
```python
import functools
import math

import jax
import jax.numpy as jnp
from jax import lax
from jax.experimental import pallas as pl
from jax.experimental.pallas import tpu as pltpu
from jax.sharding import PartitionSpec as P

WINDOWS = 8
SAMPLES = 2048
REACH = 128
TIME_HALF = 128
BIN_HALF = 32
LOCAL = 32
AHEAD = REACH // LOCAL
BLOCK = 256
ROWS = LOCAL * WINDOWS
GROUPS = 2
CHUNKS = 1
VMEM_LIMIT = 24 << 20
STEPS = 4
F32 = jnp.float32
BF16 = jnp.bfloat16
MESH = pl.DeviceIdType.MESH

SLOT_AHEAD = (0, 1, 2, 3, 8)
SLOT_BEHIND = (5, 6, 7, 4, 9)
SLOTS = 12


def iota(shape, axis):
    return lax.broadcasted_iota(jnp.int32, shape, axis)


def cos_sin(index):
    quarter = SAMPLES // 4
    turn = (index + quarter // 2) // quarter
    x = (index - turn * quarter).astype(F32) * (2.0 * math.pi / SAMPLES)
    y = x * x
    s = x * (1.0 + y * (-1 / 6 + y * (1 / 120 + y * (-1 / 5040 + y * (1 / 362880)))))
    c = 1.0 + y * (-1 / 2 + y * (1 / 24 + y * (-1 / 720 + y * (1 / 40320))))
    turn = turn & 3
    odd = (turn & 1) == 1
    cos = jnp.where(odd, s, c)
    sin = jnp.where(odd, c, s)
    cos = jnp.where((turn == 1) | (turn == 2), -cos, cos)
    sin = jnp.where(turn >= 2, -sin, sin)
    return cos, sin


def lane_bin(lane):
    block = lane // 64
    within = (lane // 32) % 2 * 16 + lane % 16
    return within + jnp.where(block == 1, -LOCAL, jnp.where(block == 2, LOCAL, 0))


def write_spread(spread_ref):
    half = BLOCK // 2
    row, lane = iota((half, half), 0), iota((half, half), 1)
    lower = (row >= lane).astype(BF16)
    upper = (row <= lane).astype(BF16)
    ones = jnp.ones((half, half), BF16)
    zeros = jnp.zeros((half, half), BF16)
    for i, pair in enumerate(((lower, zeros), (ones, lower), (upper, ones), (zeros, upper))):
        for j, piece in enumerate(pair):
            spread_ref[i * half : (i + 1) * half, j * half : (j + 1) * half] = piece


def write_band(band_ref, below, above):
    shape = (16, 128)
    target = iota(shape, 1) // 32 % 2 * 16 + iota(shape, 1) % 16
    for group in range(GROUPS):
        source = iota(shape, 0) + 16 * group
        pieces = (
            jnp.ones(shape, BF16),
            jnp.where(source >= target, below, 0.0).astype(BF16),
            jnp.where(source <= target, above, 0.0).astype(BF16),
            jnp.zeros(shape, BF16),
        )
        for block, piece in enumerate(pieces):
            for part in range(2):
                band_ref[pl.ds(block * 64 + group * 32 + part * 16, 16)] = piece


def write_table(table_ref, angle_ref, first_bin):
    row = iota((48, BLOCK), 0)
    step_of = jnp.where(row < 32, 8 * row, jnp.where(row < 40, row - 32, 256 * (row - 40)))
    bin_of = lane_bin(iota((48, BLOCK), 1)) + first_bin
    cos, sin = cos_sin((bin_of * step_of) & (SAMPLES - 1))
    scale = 1.0 / math.sqrt(SAMPLES)
    angle_ref[0] = cos[:40] * scale
    angle_ref[1] = sin[:40] * scale
    imaginary = (iota((8, BLOCK), 1) // 16) % 2 == 1
    cos1, sin1 = cos[32:40], sin[32:40]
    same_c, same_s = jnp.where(imaginary, -sin1, cos1), jnp.where(imaginary, -cos1, -sin1)
    next_c, next_s = same_s, -same_c
    cos8 = jnp.broadcast_to(cos[41:42], (16, BLOCK))
    sin8 = jnp.broadcast_to(sin[41:42], (16, BLOCK))
    quarter = (lane_bin(iota((16, BLOCK), 1)) + first_bin) & 3
    real4 = jnp.where(quarter == 0, 1.0, jnp.where(quarter == 2, -1.0, 0.0)).astype(BF16)
    imag4 = jnp.where(quarter == 1, 1.0, jnp.where(quarter == 3, -1.0, 0.0)).astype(BF16)
    sign2 = jnp.where((quarter & 1) == 0, 1.0, -1.0).astype(BF16)
    for t in range(BLOCK // 16):
        x, y = [], []
        for i in (2 * t, 2 * t + 1):
            c = jnp.broadcast_to(angle_ref[0, pl.ds(i, 1)], (8, BLOCK))
            s = jnp.broadcast_to(angle_ref[1, pl.ds(i, 1)], (8, BLOCK))
            x.append(c * same_c + s * same_s)
            y.append(c * next_c + s * next_s)
        x, y = jnp.concatenate(x, axis=0), jnp.concatenate(y, axis=0)
        for c, (u, v) in enumerate(((x, y), (x * cos8 + y * sin8, y * cos8 - x * sin8))):
            u, v = u.astype(BF16), v.astype(BF16)
            turned = u * real4 + v * imag4
            for step, value in ((c, u), (c + 2, turned), (c + 4, u * sign2), (c + 6, turned * sign2)):
                table_ref[pl.ds(step * BLOCK + 16 * t, 16)] = value


def front_kernel(
    ahead_count, freq_count, strain_ref, ok_hbm, window_hbm, gath_ref, use_ref,
    x_ref, ok_ref, window_ref, table_ref, angle_ref, spread_ref, band_ref, white_ref,
    in_sem, small_sem, use_send, use_recv, send_sem, recv_sem,
):
    me = lax.axis_index("ch")
    freq = lax.axis_index("freq")
    first_bin = freq * LOCAL + 1
    rows = ROWS // CHUNKS
    channels = LOCAL // CHUNKS

    small = [
        pltpu.make_async_copy(ok_hbm, ok_ref, small_sem.at[0]),
        pltpu.make_async_copy(window_hbm, window_ref, small_sem.at[1]),
    ]
    for load in small:
        load.start()
    loads = []
    for chunk in range(CHUNKS):
        part = pl.ds(chunk * rows, rows)
        loads.append(pltpu.make_async_copy(strain_ref.at[part], x_ref.at[part], in_sem.at[chunk]))
        loads[-1].start()

    barrier = pltpu.get_barrier_semaphore()
    peers = jnp.int32(0)
    for distance in range(1, AHEAD + 1):
        for step in (distance, -distance):
            there = (me + step >= 0) & (me + step < ahead_count)
            peers = peers + there.astype(jnp.int32)

            @pl.when(there)
            def _():
                pl.semaphore_signal(barrier, 1, device_id={"ch": me + step}, device_id_type=MESH)

    write_table(table_ref, angle_ref, first_bin)
    write_spread(spread_ref)
    write_band(band_ref, (freq > 0).astype(F32), (freq < freq_count - 1).astype(F32))

    for slot in range(10, SLOTS):
        gath_ref[slot] = jnp.zeros((LOCAL, 512), BF16)
        use_ref[slot] = jnp.zeros((LOCAL, 128), BF16)

    @pl.when((me < AHEAD) | (me >= ahead_count - AHEAD))
    def _():
        for distance in range(1, AHEAD + 1):
            for step, slot in ((distance, SLOT_AHEAD[distance]), (-distance, SLOT_BEHIND[distance])):

                @pl.when((me + step < 0) | (me + step >= ahead_count))
                def _():
                    gath_ref[slot] = jnp.zeros((LOCAL, 512), BF16)
                    use_ref[slot] = jnp.zeros((LOCAL, 128), BF16)

    for load in small:
        load.wait()
    usable8 = (window_ref[...].astype(F32) * ok_ref[...].astype(F32)).astype(BF16)
    widen = (iota((WINDOWS, 128), 0) == iota((WINDOWS, 128), 1)).astype(BF16)
    usable = lax.dot_general(usable8, widen, (((0,), (0,)), ((), ())), preferred_element_type=F32).astype(BF16)
    flip = (iota((LOCAL, LOCAL), 0) + iota((LOCAL, LOCAL), 1) == LOCAL - 1).astype(BF16)
    use_ref[SLOT_AHEAD[0]] = usable
    use_ref[SLOT_BEHIND[0]] = jnp.dot(flip, usable, preferred_element_type=F32).astype(BF16)
    keep = []
    for half in range(2):
        expand = (iota((128, 128), 0) == 4 * half + iota((128, 128), 1) // 32).astype(BF16)
        keep.append(jnp.dot(usable, expand, preferred_element_type=F32))

    pl.semaphore_wait(barrier, peers)

    def copies(step, part):
        own, slot = (SLOT_BEHIND[0], SLOT_BEHIND[step]) if step > 0 else (SLOT_AHEAD[0], SLOT_AHEAD[-step])
        which = (step + AHEAD) if step < 0 else (step + AHEAD - 1)
        if part is None:
            src, dst, send, recv = use_ref.at[own], use_ref.at[slot], use_send.at[which], use_recv.at[which]
        else:
            at = pl.ds((CHUNKS - 1 - part if step > 0 else part) * channels, channels)
            src, dst = gath_ref.at[own, at], gath_ref.at[slot, at]
            send, recv = send_sem.at[part, which], recv_sem.at[part, which]
        return pltpu.make_async_remote_copy(
            src_ref=src, dst_ref=dst, send_sem=send, recv_sem=recv, device_id={"ch": me + step}, device_id_type=MESH
        )

    steps = [s * d for d in range(AHEAD, 0, -1) for s in (1, -1)]

    def for_each(part, act):
        for step in steps:
            @pl.when((me + step >= 0) & (me + step < ahead_count))
            def _():
                act(copies(step, part))

    def for_each_source(part, act):
        for step in steps:
            @pl.when((me - step >= 0) & (me - step < ahead_count))
            def _():
                act(copies(step, part))

    for_each(None, lambda copy: copy.start())

    lanes = iota((channels, 128), 1) // 32
    flip = (iota((channels, channels), 0) + iota((channels, channels), 1) == channels - 1).astype(BF16)
    for chunk in range(CHUNKS):
        loads[chunk].wait()
        part = pl.ds(chunk * rows, rows)
        spectrum = jnp.zeros((rows, BLOCK), F32)
        for block in range(SAMPLES // BLOCK):
            low = max(block * BLOCK - TIME_HALF, 0)
            high = min(block * BLOCK + BLOCK + TIME_HALF, SAMPLES)
            skip = low - (block * BLOCK - TIME_HALF)
            sums = jnp.dot(
                jnp.abs(x_ref[part, low:high]), spread_ref[skip : skip + high - low], preferred_element_type=F32
            )
            level = sums * (1.0 / (2 * TIME_HALF + 1)) + 1e-06
            leveled = (x_ref[part, block * BLOCK : (block + 1) * BLOCK].astype(F32) / level).astype(BF16)
            spectrum = spectrum + jnp.dot(
                leveled, table_ref[block * BLOCK : (block + 1) * BLOCK], preferred_element_type=F32
            )
        power = spectrum * spectrum
        coarse = power.astype(BF16)
        fine = (power - coarse.astype(F32)).astype(BF16)
        smooth = jnp.dot(coarse, band_ref[...], preferred_element_type=F32) + jnp.dot(
            fine, band_ref[...], preferred_element_type=F32
        )
        white_ref[part] = spectrum[:, :128] * lax.rsqrt(smooth * (1.0 / (2 * BIN_HALF + 1)) + 1e-06)
        at = chunk * channels
        by_window = [white_ref[pl.ds(chunk * rows + w, channels, stride=WINDOWS)] for w in range(WINDOWS)]
        for group in range(GROUPS):
            for half in range(2):
                piece = None
                for i in range(4):
                    moved = pltpu.roll(by_window[4 * half + i], (32 * (i - group)) % 128, 1)
                    piece = moved if piece is None else jnp.where(lanes == i, moved, piece)
                piece = (piece * keep[half][at : at + channels]).astype(BF16)
                where = pl.ds((2 * group + half) * 128, 128)
                gath_ref[SLOT_AHEAD[0], pl.ds(at, channels), where] = piece
                gath_ref[SLOT_BEHIND[0], pl.ds(LOCAL - at - channels, channels), where] = jnp.dot(
                    flip, piece, preferred_element_type=F32
                ).astype(BF16)
        for_each(chunk, lambda copy: copy.start())

    for part in (None, *range(CHUNKS)):
        for_each_source(part, lambda copy: copy.wait_recv())
        for_each(part, lambda copy: copy.wait_send())


def front(strain, channel_ok, window_ok, ahead_count, freq_count):
    hbm = pl.BlockSpec(memory_space=pltpu.MemorySpace.HBM)
    vmem = pl.BlockSpec(memory_space=pltpu.VMEM)
    args = (strain.reshape(ROWS, SAMPLES), channel_ok.reshape(1, LOCAL), window_ok.T)
    return pl.pallas_call(
        functools.partial(front_kernel, ahead_count, freq_count),
        out_shape=(
            jax.ShapeDtypeStruct((SLOTS, LOCAL, 512), BF16),
            jax.ShapeDtypeStruct((SLOTS, LOCAL, 128), BF16),
        ),
        in_specs=[hbm, hbm, hbm],
        out_specs=(vmem, vmem),
        scratch_shapes=[
            pltpu.VMEM((ROWS, SAMPLES), BF16),
            pltpu.VMEM((1, LOCAL), jnp.int32),
            pltpu.VMEM((WINDOWS, LOCAL), jnp.int32),
            pltpu.VMEM((SAMPLES, BLOCK), BF16),
            pltpu.VMEM((2, 40, BLOCK), F32),
            pltpu.VMEM((2 * BLOCK, BLOCK), BF16),
            pltpu.VMEM((BLOCK, 128), BF16),
            pltpu.VMEM((ROWS, 128), F32),
            pltpu.SemaphoreType.DMA((CHUNKS,)),
            pltpu.SemaphoreType.DMA((2,)),
            pltpu.SemaphoreType.DMA((2 * AHEAD,)),
            pltpu.SemaphoreType.DMA((2 * AHEAD,)),
            pltpu.SemaphoreType.DMA((CHUNKS, 2 * AHEAD)),
            pltpu.SemaphoreType.DMA((CHUNKS, 2 * AHEAD)),
        ],
        compiler_params=pltpu.CompilerParams(collective_id=0, has_side_effects=True, vmem_limit_bytes=VMEM_LIMIT),
        name="front",
    )(*(pltpu.with_memory_space_constraint(arg, pltpu.HBM) for arg in args))


def lag_rows(ahead, behind, tail):
    row = iota((LOCAL, 128), 0)
    lane = iota((LOCAL, 128), 1)
    ahead = jnp.where(lane <= row, tail, ahead)
    behind = jnp.where((lane >= 32) & (lane < 64 - row), tail, behind)
    return (
        jnp.take_along_axis(ahead, (lane + row + 1) & 127, axis=1),
        pltpu.roll(behind, 64, 1, stride=1, stride_axis=0),
    )


def cross_kernel(gath_ref, use_ref, ahead_hbm, behind_hbm, ahead_ref, behind_ref, out_sem):
    contract = (((1,), (1,)), ((), ()))
    per_step = LOCAL // STEPS
    pairs = lax.dot_general(use_ref[0], use_ref[...].reshape(SLOTS * LOCAL, 128), contract, preferred_element_type=F32)
    scales = [1.0 / jnp.maximum(n, 1.0) for n in lag_rows(pairs[:, :128], pairs[:, 128:256], pairs[:, 256:])]
    lane_of = iota((LOCAL, 256), 1) % 16
    imaginary = (iota((LOCAL, 256), 1) // 16) % 2 == 1
    copies = []
    for step in range(STEPS):
        group, first = divmod(step * per_step, 16)
        at = slice(group * 256, (group + 1) * 256)
        own = gath_ref[0, :, at]
        wide = own.astype(F32)
        swap = jnp.where(imaginary, pltpu.roll(wide, 16, 1), -pltpu.roll(wide, 240, 1)).astype(BF16)
        lhs = jnp.concatenate(
            [
                jnp.where(lane_of == first + f, value, jnp.zeros_like(value))
                for value in (own, swap)
                for f in range(per_step)
            ],
            axis=0,
        )
        rhs = gath_ref[:, :, at].reshape(SLOTS * LOCAL, 256)
        cross = lax.dot_general(lhs, rhs, contract, preferred_element_type=F32)
        for part in range(2):
            for f in range(per_step):
                rows = slice((part * per_step + f) * LOCAL, (part * per_step + f + 1) * LOCAL)
                ahead, behind = lag_rows(cross[rows, :128], cross[rows, 128:256], cross[rows, 256:])
                ahead_ref[part, step * per_step + f] = (ahead * scales[0]).astype(BF16)
                behind_ref[part, step * per_step + f] = (behind * scales[1]).astype(BF16)
        done = pl.ds(step * per_step, per_step)
        for side, (src, dst) in enumerate(((ahead_ref, ahead_hbm), (behind_ref, behind_hbm))):
            copies.append(pltpu.make_async_copy(src.at[:, done], dst.at[:, done], out_sem.at[side, step]))
            copies[-1].start()
    for copy in copies:
        copy.wait()


def cross(gathered, usable):
    shape = (2, LOCAL, LOCAL, REACH)
    vmem = pl.BlockSpec(memory_space=pltpu.VMEM)
    hbm = pl.BlockSpec(memory_space=pltpu.MemorySpace.HBM)
    return pl.pallas_call(
        cross_kernel,
        out_shape=(jax.ShapeDtypeStruct(shape, BF16), jax.ShapeDtypeStruct(shape, BF16)),
        in_specs=[vmem, vmem],
        out_specs=(hbm, hbm),
        scratch_shapes=[pltpu.VMEM(shape, BF16), pltpu.VMEM(shape, BF16), pltpu.SemaphoreType.DMA((2, STEPS))],
        compiler_params=pltpu.CompilerParams(vmem_limit_bytes=VMEM_LIMIT),
        name="cross",
    )(gathered, usable)


def solution(mesh):
    ahead_count = mesh.shape["ch"]
    freq_count = mesh.shape["freq"]

    def per_device(strain, channel_ok, window_ok):
        gathered, usable = front(strain, channel_ok, window_ok, ahead_count, freq_count)
        return cross(gathered, usable)

    return jax.shard_map(
        per_device,
        mesh=mesh,
        in_specs=(P("ch", None, None), P("ch"), P("ch", None)),
        out_specs=(P(None, "freq", "ch", None), P(None, "freq", "ch", None)),
        check_vma=False,
    )
```

time: 23.6 us -> 18.6 us (0.79)
  the two profiles are of different devices: /device:TPU:256 before, /device:TPU:262 now
where the time goes in v2:
time: 18.6 us; the launch traced here: 18.5 us
  Pallas kernels  17.9 us (96%)
  between operations  0.64 us (3%)
    pallas_call x1, Pallas kernels, front(): pl.pallas_call(functools.partial(front_kernel, ahead_count, freq_count),...  15.8 us
    pallas_call x1, Pallas kernels, cross(): pl.pallas_call(cross_kernel, out_shape=(jax.ShapeDtypeStruct(shape, BF16)...  2.09 us

profile of v2, /device:TPU:262, one launch (start us, length us, event | category | flops | bytes accessed | tf_op | source)
XLA Modules:
  0.0 18.5 jit_solution(8194620050384196380)
XLA Ops:
  0.6 15.8 %front.1 = (bf16[12,32,512]{2,1,0:T(8,128)(2,1)S(1)}, bf16[12,32,128]{2,1,0:T(8,128)(2,1)S(1)}) custom-call(bf16[256,2048]{1,0:T(8,128)(2,1)} %bitcast.3, s32[1,32]{1,0:T(1,128)} %bitcast.5, s32[8,32]{1,0:T(8,128)} %bitcast.4), custom_call_target="tpu_custom_call" | custom-call | tf_op jit(solution)/shard_map/front/pallas_call | solution.py:266
  16.4 2.1 %cross.1 = (bf16[2,32,32,128]{3,2,1,0:T(8,128)(2,1)}, bf16[2,32,32,128]{3,2,1,0:T(8,128)(2,1)}) custom-call(bf16[12,32,512]{2,1,0:T(8,128)(2,1)S(1)} %get-tuple-element.4.gath_ref, bf16[12,32,128]{2,1,0:T(8,128)(2,1)S(1)} %get-tuple-element.5.use_ref), custom_call_target="tpu_custom_call" | custom-call | tf_op jit(solution)/shard_map/cross/pallas_call | solution.py:348

commit v3 on v2

v3 whole, which is shorter than its diff:
```python
import functools
import math

import jax
import jax.numpy as jnp
from jax import lax
from jax.experimental import pallas as pl
from jax.experimental.pallas import tpu as pltpu
from jax.sharding import PartitionSpec as P

WINDOWS = 8
SAMPLES = 2048
REACH = 128
TIME_HALF = 128
BIN_HALF = 32
LOCAL = 32
AHEAD = REACH // LOCAL
BLOCK = 256
ROWS = LOCAL * WINDOWS
GROUPS = 2
TALL = 4 * LOCAL + WINDOWS
VMEM_LIMIT = 24 << 20
STEPS = 4
F32 = jnp.float32
BF16 = jnp.bfloat16
MESH = pl.DeviceIdType.MESH

SLOT_AHEAD = (0, 1, 2, 3, 8)
SLOT_BEHIND = (5, 6, 7, 4, 9)
SLOTS = 12


def iota(shape, axis):
    return lax.broadcasted_iota(jnp.int32, shape, axis)


def cos_sin(index):
    quarter = SAMPLES // 4
    turn = (index + quarter // 2) // quarter
    x = (index - turn * quarter).astype(F32) * (2.0 * math.pi / SAMPLES)
    y = x * x
    s = x * (1.0 + y * (-1 / 6 + y * (1 / 120 + y * (-1 / 5040 + y * (1 / 362880)))))
    c = 1.0 + y * (-1 / 2 + y * (1 / 24 + y * (-1 / 720 + y * (1 / 40320))))
    turn = turn & 3
    odd = (turn & 1) == 1
    cos = jnp.where(odd, s, c)
    sin = jnp.where(odd, c, s)
    cos = jnp.where((turn == 1) | (turn == 2), -cos, cos)
    sin = jnp.where(turn >= 2, -sin, sin)
    return cos, sin


def lane_bin(lane):
    block = lane // 64
    within = (lane // 32) % 2 * 16 + lane % 16
    return within + jnp.where(block == 1, -LOCAL, jnp.where(block == 2, LOCAL, 0))


def write_spread(spread_ref):
    half = BLOCK // 2
    row, lane = iota((half, half), 0), iota((half, half), 1)
    lower = (row >= lane).astype(BF16)
    upper = (row <= lane).astype(BF16)
    ones = jnp.ones((half, half), BF16)
    zeros = jnp.zeros((half, half), BF16)
    for i, pair in enumerate(((lower, zeros), (ones, lower), (upper, ones), (zeros, upper))):
        for j, piece in enumerate(pair):
            spread_ref[i * half : (i + 1) * half, j * half : (j + 1) * half] = piece


def write_band(band_ref, below, above):
    shape = (16, 128)
    target = iota(shape, 1) // 32 % 2 * 16 + iota(shape, 1) % 16
    for group in range(GROUPS):
        source = iota(shape, 0) + 16 * group
        pieces = (
            jnp.ones(shape, BF16),
            jnp.where(source >= target, below, 0.0).astype(BF16),
            jnp.where(source <= target, above, 0.0).astype(BF16),
            jnp.zeros(shape, BF16),
        )
        for block, piece in enumerate(pieces):
            for part in range(2):
                band_ref[pl.ds(block * 64 + group * 32 + part * 16, 16)] = piece


def write_table(table_ref, angle_ref, first_bin):
    row = iota((48, BLOCK), 0)
    step_of = jnp.where(row < 32, 8 * row, jnp.where(row < 40, row - 32, 256 * (row - 40)))
    bin_of = lane_bin(iota((48, BLOCK), 1)) + first_bin
    cos, sin = cos_sin((bin_of * step_of) & (SAMPLES - 1))
    scale = 1.0 / math.sqrt(SAMPLES)
    angle_ref[0] = cos[:40] * scale
    angle_ref[1] = sin[:40] * scale
    imaginary = (iota((8, BLOCK), 1) // 16) % 2 == 1
    cos1, sin1 = cos[32:40], sin[32:40]
    same_c, same_s = jnp.where(imaginary, -sin1, cos1), jnp.where(imaginary, -cos1, -sin1)
    next_c, next_s = same_s, -same_c
    cos8 = jnp.broadcast_to(cos[41:42], (16, BLOCK))
    sin8 = jnp.broadcast_to(sin[41:42], (16, BLOCK))
    quarter = (lane_bin(iota((16, BLOCK), 1)) + first_bin) & 3
    real4 = jnp.where(quarter == 0, 1.0, jnp.where(quarter == 2, -1.0, 0.0)).astype(BF16)
    imag4 = jnp.where(quarter == 1, 1.0, jnp.where(quarter == 3, -1.0, 0.0)).astype(BF16)
    sign2 = jnp.where((quarter & 1) == 0, 1.0, -1.0).astype(BF16)
    for t in range(BLOCK // 16):
        x, y = [], []
        for i in (2 * t, 2 * t + 1):
            c = jnp.broadcast_to(angle_ref[0, pl.ds(i, 1)], (8, BLOCK))
            s = jnp.broadcast_to(angle_ref[1, pl.ds(i, 1)], (8, BLOCK))
            x.append(c * same_c + s * same_s)
            y.append(c * next_c + s * next_s)
        x, y = jnp.concatenate(x, axis=0), jnp.concatenate(y, axis=0)
        for c, (u, v) in enumerate(((x, y), (x * cos8 + y * sin8, y * cos8 - x * sin8))):
            u, v = u.astype(BF16), v.astype(BF16)
            turned = u * real4 + v * imag4
            for step, value in ((c, u), (c + 2, turned), (c + 4, u * sign2), (c + 6, turned * sign2)):
                table_ref[pl.ds(step * BLOCK + 16 * t, 16)] = value


def lag_rows(ahead, behind, tail):
    row = iota((LOCAL, 128), 0)
    lane = iota((LOCAL, 128), 1)
    ahead = jnp.where(lane <= row, tail, ahead)
    behind = jnp.where((lane >= 32) & (lane < 64 - row), tail, behind)
    return (
        jnp.take_along_axis(ahead, (lane + row + 1) & 127, axis=1),
        pltpu.roll(behind, 64, 1, stride=1, stride_axis=0),
    )


def front_kernel(
    ahead_count, freq_count, strain_ref, ok_hbm, window_hbm, gath_ref,
    x_ref, ok_ref, window_ref, table_ref, angle_ref, spread_ref, band_ref, white_ref,
    in_sem, small_sem, send_sem, recv_sem,
):
    me = lax.axis_index("ch")
    freq = lax.axis_index("freq")
    first_bin = freq * LOCAL + 1

    small = [
        pltpu.make_async_copy(ok_hbm, ok_ref, small_sem.at[0]),
        pltpu.make_async_copy(window_hbm, window_ref, small_sem.at[1]),
    ]
    for load in small:
        load.start()
    load_strain = pltpu.make_async_copy(strain_ref, x_ref, in_sem)
    load_strain.start()

    core = me % 2
    partner = me + 1 - 2 * core
    exists = lambda other: (other >= 0) & (other < ahead_count)
    barrier = pltpu.get_barrier_semaphore()
    peers = jnp.int32(1)
    pl.semaphore_signal(barrier, 1, device_id={"ch": partner}, device_id_type=MESH)
    for step in (4, -4, 2, -2):
        peers = peers + exists(me + step).astype(jnp.int32)

        @pl.when(exists(me + step))
        def _():
            pl.semaphore_signal(barrier, 1, device_id={"ch": me + step}, device_id_type=MESH)

    write_table(table_ref, angle_ref, first_bin)
    write_spread(spread_ref)
    write_band(band_ref, (freq > 0).astype(F32), (freq < freq_count - 1).astype(F32))

    for slot in range(10, SLOTS):
        gath_ref[slot] = jnp.zeros((TALL, 128), BF16)

    @pl.when((me < AHEAD) | (me >= ahead_count - AHEAD))
    def _():
        for distance in range(1, AHEAD + 1):
            for step, slot in ((distance, SLOT_AHEAD[distance]), (-distance, SLOT_BEHIND[distance])):

                @pl.when((me + step < 0) | (me + step >= ahead_count))
                def _():
                    gath_ref[slot] = jnp.zeros((TALL, 128), BF16)

    for load in small:
        load.wait()
    usable = (window_ref[...].astype(F32) * ok_ref[...].astype(F32)).astype(BF16)
    lane = iota((LOCAL, 128), 1)
    channel = iota((LOCAL, 128), 0)
    for slot, at in ((SLOT_AHEAD[0], channel), (SLOT_BEHIND[0], LOCAL - 1 - channel)):
        spread = jnp.dot(usable, (lane == at).astype(BF16), preferred_element_type=F32)
        gath_ref[slot, pl.ds(4 * LOCAL, WINDOWS)] = spread.astype(BF16)
    keep = []
    for half in range(2):
        expand = (iota((WINDOWS, 128), 0) == 4 * half + iota((WINDOWS, 128), 1) // 32).astype(BF16)
        keep.append(lax.dot_general(usable, expand, (((0,), (0,)), ((), ())), preferred_element_type=F32))

    load_strain.wait()
    spectrum = jnp.zeros((ROWS, BLOCK), F32)
    for block in range(SAMPLES // BLOCK):
        low = max(block * BLOCK - TIME_HALF, 0)
        high = min(block * BLOCK + BLOCK + TIME_HALF, SAMPLES)
        skip = low - (block * BLOCK - TIME_HALF)
        sums = jnp.dot(
            jnp.abs(x_ref[:, low:high]), spread_ref[skip : skip + high - low], preferred_element_type=F32
        )
        level = sums * (1.0 / (2 * TIME_HALF + 1)) + 1e-06
        leveled = (x_ref[:, block * BLOCK : (block + 1) * BLOCK].astype(F32) / level).astype(BF16)
        spectrum = spectrum + jnp.dot(
            leveled, table_ref[block * BLOCK : (block + 1) * BLOCK], preferred_element_type=F32
        )
    power = spectrum * spectrum
    coarse = power.astype(BF16)
    fine = (power - coarse.astype(F32)).astype(BF16)
    smooth = jnp.dot(coarse, band_ref[...], preferred_element_type=F32) + jnp.dot(
        fine, band_ref[...], preferred_element_type=F32
    )
    white_ref[...] = spectrum[:, :128] * lax.rsqrt(smooth * (1.0 / (2 * BIN_HALF + 1)) + 1e-06)
    by_window = [white_ref[pl.ds(w, LOCAL, stride=WINDOWS)] for w in range(WINDOWS)]
    lanes = iota((LOCAL, 128), 1) // 32
    flip = (iota((LOCAL, LOCAL), 0) + iota((LOCAL, LOCAL), 1) == LOCAL - 1).astype(BF16)
    for group in range(GROUPS):
        for half in range(2):
            piece = None
            for i in range(4):
                moved = pltpu.roll(by_window[4 * half + i], (32 * (i - group)) % 128, 1)
                piece = moved if piece is None else jnp.where(lanes == i, moved, piece)
            piece = (piece * keep[half]).astype(BF16)
            where = pl.ds((2 * group + half) * LOCAL, LOCAL)
            gath_ref[SLOT_AHEAD[0], where] = piece
            gath_ref[SLOT_BEHIND[0], where] = jnp.dot(flip, piece, preferred_element_type=F32).astype(BF16)

    pick = lambda even, odd: jnp.where(core == 0, even, odd)

    def copy(src, dst, which, recv, target):
        return pltpu.make_async_remote_copy(
            src_ref=gath_ref.at[src], dst_ref=gath_ref.at[dst], send_sem=send_sem.at[which],
            recv_sem=recv_sem.at[recv], device_id={"ch": target}, device_id_type=MESH,
        )

    own_sends = [
        (SLOT_BEHIND[0], SLOT_BEHIND[4], 7, me + 4),
        (SLOT_AHEAD[0], SLOT_AHEAD[4], 3, me - 4),
        (SLOT_BEHIND[0], SLOT_BEHIND[2], 5, me + 2),
        (SLOT_AHEAD[0], SLOT_AHEAD[2], 1, me - 2),
        (pick(SLOT_BEHIND[0], SLOT_AHEAD[0]), pick(SLOT_BEHIND[1], SLOT_AHEAD[1]), pick(4, 0), partner),
    ]
    passes = [
        (SLOT_BEHIND[2], pick(SLOT_BEHIND[3], SLOT_BEHIND[1]), 5, pick(6, 4), me - 2),
        (SLOT_AHEAD[2], pick(SLOT_AHEAD[1], SLOT_AHEAD[3]), 1, pick(0, 2), me + 2),
        (pick(SLOT_AHEAD[4], SLOT_BEHIND[4]), pick(SLOT_AHEAD[3], SLOT_BEHIND[3]), pick(3, 7), pick(2, 6), me + pick(4, -4)),
    ]
    pl.semaphore_wait(barrier, peers)
    for which, (src, dst, recv, target) in enumerate(own_sends):
        @pl.when(exists(target))
        def _():
            copy(src, dst, which, recv, target).start()
    for i, (src, dst, mine, recv, source) in enumerate(passes):
        @pl.when(exists(source))
        def _():
            copy(src, src, 0, mine, partner).wait_recv()
            copy(src, dst, 5 + i, recv, partner).start()

    for slot, mine, source in (
        (pick(SLOT_BEHIND[4], SLOT_AHEAD[4]), pick(7, 3), me - pick(4, -4)),
        (pick(SLOT_AHEAD[1], SLOT_BEHIND[1]), pick(0, 4), partner),
        (pick(SLOT_BEHIND[1], SLOT_AHEAD[1]), pick(4, 0), me - pick(1, -1)),
        (SLOT_AHEAD[3], 2, me + 3),
        (SLOT_BEHIND[3], 6, me - 3),
    ):
        @pl.when(exists(source))
        def _():
            copy(slot, slot, 0, mine, partner).wait_recv()
    for which, (src, dst, recv, target) in enumerate(own_sends):
        @pl.when(exists(target))
        def _():
            copy(src, dst, which, recv, target).wait_send()
    for i, (src, dst, mine, recv, source) in enumerate(passes):
        @pl.when(exists(source))
        def _():
            copy(src, dst, 5 + i, recv, partner).wait_send()


def front(strain, channel_ok, window_ok, ahead_count, freq_count):
    hbm = pl.BlockSpec(memory_space=pltpu.MemorySpace.HBM)
    vmem = pl.BlockSpec(memory_space=pltpu.VMEM)
    args = (strain.reshape(ROWS, SAMPLES), channel_ok.reshape(1, LOCAL), window_ok.T)
    return pl.pallas_call(
        functools.partial(front_kernel, ahead_count, freq_count),
        out_shape=jax.ShapeDtypeStruct((SLOTS, TALL, 128), BF16),
        in_specs=[hbm, hbm, hbm],
        out_specs=vmem,
        scratch_shapes=[
            pltpu.VMEM((ROWS, SAMPLES), BF16),
            pltpu.VMEM((1, LOCAL), jnp.int32),
            pltpu.VMEM((WINDOWS, LOCAL), jnp.int32),
            pltpu.VMEM((SAMPLES, BLOCK), BF16),
            pltpu.VMEM((2, 40, BLOCK), F32),
            pltpu.VMEM((2 * BLOCK, BLOCK), BF16),
            pltpu.VMEM((BLOCK, 128), BF16),
            pltpu.VMEM((ROWS, 128), F32),
            pltpu.SemaphoreType.DMA,
            pltpu.SemaphoreType.DMA((2,)),
            pltpu.SemaphoreType.DMA((8,)),
            pltpu.SemaphoreType.DMA((8,)),
        ],
        compiler_params=pltpu.CompilerParams(collective_id=0, has_side_effects=True, vmem_limit_bytes=VMEM_LIMIT),
        name="front",
    )(*(pltpu.with_memory_space_constraint(arg, pltpu.HBM) for arg in args))


def cross_kernel(gath_ref, ahead_hbm, behind_hbm, ahead_ref, behind_ref, out_sem):
    contract = (((1,), (1,)), ((), ()))
    per_step = LOCAL // STEPS
    use = [gath_ref[slot, pl.ds(4 * LOCAL, WINDOWS)].astype(F32) for slot in range(10)]
    beside = []
    for tile in range(3):
        moved = [pltpu.roll(use[slot], LOCAL * (slot % 4), 1) for slot in range(4 * tile, min(4 * tile + 4, 10))]
        beside.append(functools.reduce(jnp.add, moved).astype(BF16))
    pairs = lax.dot_general(
        use[0][:, :LOCAL].astype(BF16), jnp.concatenate(beside, axis=1), (((0,), (0,)), ((), ())), preferred_element_type=F32
    )
    scales = [1.0 / jnp.maximum(n, 1.0) for n in lag_rows(pairs[:, :128], pairs[:, 128:256], pairs[:, 256:])]
    lane_of = iota((LOCAL, 256), 1) % 16
    imaginary = (iota((LOCAL, 256), 1) // 16) % 2 == 1
    copies = []
    for step in range(STEPS):
        group, first = divmod(step * per_step, 16)
        low, high = (pl.ds((2 * group + half) * LOCAL, LOCAL) for half in range(2))
        own = jnp.concatenate([gath_ref[0, low], gath_ref[0, high]], axis=1)
        wide = own.astype(F32)
        swap = jnp.where(imaginary, pltpu.roll(wide, 16, 1), -pltpu.roll(wide, 240, 1)).astype(BF16)
        lhs = jnp.concatenate(
            [
                jnp.where(lane_of == first + f, value, jnp.zeros_like(value))
                for value in (own, swap)
                for f in range(per_step)
            ],
            axis=0,
        )
        rhs = jnp.concatenate([gath_ref[:, part].reshape(SLOTS * LOCAL, 128) for part in (low, high)], axis=1)
        cross = lax.dot_general(lhs, rhs, contract, preferred_element_type=F32)
        for part in range(2):
            for f in range(per_step):
                rows = slice((part * per_step + f) * LOCAL, (part * per_step + f + 1) * LOCAL)
                ahead, behind = lag_rows(cross[rows, :128], cross[rows, 128:256], cross[rows, 256:])
                ahead_ref[part, step * per_step + f] = (ahead * scales[0]).astype(BF16)
                behind_ref[part, step * per_step + f] = (behind * scales[1]).astype(BF16)
        done = pl.ds(step * per_step, per_step)
        for side, (src, dst) in enumerate(((ahead_ref, ahead_hbm), (behind_ref, behind_hbm))):
            copies.append(pltpu.make_async_copy(src.at[:, done], dst.at[:, done], out_sem.at[side, step]))
            copies[-1].start()
    for copy in copies:
        copy.wait()


def cross(gathered):
    shape = (2, LOCAL, LOCAL, REACH)
    vmem = pl.BlockSpec(memory_space=pltpu.VMEM)
    hbm = pl.BlockSpec(memory_space=pltpu.MemorySpace.HBM)
    return pl.pallas_call(
        cross_kernel,
        out_shape=(jax.ShapeDtypeStruct(shape, BF16), jax.ShapeDtypeStruct(shape, BF16)),
        in_specs=[vmem],
        out_specs=(hbm, hbm),
        scratch_shapes=[pltpu.VMEM(shape, BF16), pltpu.VMEM(shape, BF16), pltpu.SemaphoreType.DMA((2, STEPS))],
        compiler_params=pltpu.CompilerParams(vmem_limit_bytes=VMEM_LIMIT),
        name="cross",
    )(gathered)


def solution(mesh):
    ahead_count = mesh.shape["ch"]
    freq_count = mesh.shape["freq"]

    def per_device(strain, channel_ok, window_ok):
        gathered = front(strain, channel_ok, window_ok, ahead_count, freq_count)
        return cross(gathered)

    return jax.shard_map(
        per_device,
        mesh=mesh,
        in_specs=(P("ch", None, None), P("ch"), P("ch", None)),
        out_specs=(P(None, "freq", "ch", None), P(None, "freq", "ch", None)),
        check_vma=False,
    )
```

time: 18.6 us -> 16.4 us (0.88)
  the two profiles are of different devices: /device:TPU:262 before, /device:TPU:189 now
where the time goes in v3:
time: 16.4 us; the launch traced here: 16.2 us
  Pallas kernels  15.6 us (95%)
  between operations  0.64 us (4%)
    pallas_call x1, Pallas kernels, front(): pl.pallas_call(functools.partial(front_kernel, ahead_count, freq_count),...  13.4 us
    pallas_call x1, Pallas kernels, cross(): pl.pallas_call(cross_kernel, out_shape=(jax.ShapeDtypeStruct(shape, BF16)...  2.14 us

profile of v3, /device:TPU:189, one launch (start us, length us, event | category | flops | bytes accessed | tf_op | source)
XLA Modules:
  0.0 16.2 jit_solution(12146132828821120310)
XLA Ops:
  0.6 13.4 %front.1.gath_ref = bf16[12,136,128]{2,1,0:T(8,128)(2,1)S(1)} custom-call(bf16[256,2048]{1,0:T(8,128)(2,1)} %bitcast.3, s32[1,32]{1,0:T(1,128)} %bitcast.5, s32[8,32]{1,0:T(8,128)} %bitcast.4), custom_call_target="tpu_custom_call" | custom-call | tf_op jit(solution)/shard_map/front/pallas_call | solution.py:281
  14.1 2.1 %cross.1 = (bf16[2,32,32,128]{3,2,1,0:T(8,128)(2,1)}, bf16[2,32,32,128]{3,2,1,0:T(8,128)(2,1)}) custom-call(bf16[12,136,128]{2,1,0:T(8,128)(2,1)S(1)} %front.1.gath_ref), custom_call_target="tpu_custom_call" | custom-call | tf_op jit(solution)/shard_map/cross/pallas_call | solution.py:354

commit v4 on v3

--- a/solution.py
+++ b/solution.py
@@ -18,6 +18,7 @@
 BLOCK = 256
 ROWS = LOCAL * WINDOWS
 GROUPS = 2
+RING = 16
 TALL = 4 * LOCAL + WINDOWS
 VMEM_LIMIT = 24 << 20
 STEPS = 4
@@ -84,24 +85,29 @@
                 band_ref[pl.ds(block * 64 + group * 32 + part * 16, 16)] = piece
 
 
-def write_table(table_ref, angle_ref, first_bin):
+def table_parts(angle_ref, first_bin):
     row = iota((48, BLOCK), 0)
     step_of = jnp.where(row < 32, 8 * row, jnp.where(row < 40, row - 32, 256 * (row - 40)))
     bin_of = lane_bin(iota((48, BLOCK), 1)) + first_bin
     cos, sin = cos_sin((bin_of * step_of) & (SAMPLES - 1))
     scale = 1.0 / math.sqrt(SAMPLES)
-    angle_ref[0] = cos[:40] * scale
-    angle_ref[1] = sin[:40] * scale
+    angle_ref[0] = cos[:32] * scale
+    angle_ref[1] = sin[:32] * scale
     imaginary = (iota((8, BLOCK), 1) // 16) % 2 == 1
     cos1, sin1 = cos[32:40], sin[32:40]
     same_c, same_s = jnp.where(imaginary, -sin1, cos1), jnp.where(imaginary, -cos1, -sin1)
-    next_c, next_s = same_s, -same_c
     cos8 = jnp.broadcast_to(cos[41:42], (16, BLOCK))
     sin8 = jnp.broadcast_to(sin[41:42], (16, BLOCK))
     quarter = (lane_bin(iota((16, BLOCK), 1)) + first_bin) & 3
     real4 = jnp.where(quarter == 0, 1.0, jnp.where(quarter == 2, -1.0, 0.0)).astype(BF16)
     imag4 = jnp.where(quarter == 1, 1.0, jnp.where(quarter == 3, -1.0, 0.0)).astype(BF16)
     sign2 = jnp.where((quarter & 1) == 0, 1.0, -1.0).astype(BF16)
+    return same_c, same_s, cos8, sin8, real4, imag4, sign2
+
+
+def write_table(table_ref, angle_ref, parts, odd):
+    same_c, same_s, cos8, sin8, real4, imag4, sign2 = parts
+    next_c, next_s = same_s, -same_c
     for t in range(BLOCK // 16):
         x, y = [], []
         for i in (2 * t, 2 * t + 1):
@@ -110,11 +116,12 @@
             x.append(c * same_c + s * same_s)
             y.append(c * next_c + s * next_s)
         x, y = jnp.concatenate(x, axis=0), jnp.concatenate(y, axis=0)
-        for c, (u, v) in enumerate(((x, y), (x * cos8 + y * sin8, y * cos8 - x * sin8))):
-            u, v = u.astype(BF16), v.astype(BF16)
-            turned = u * real4 + v * imag4
-            for step, value in ((c, u), (c + 2, turned), (c + 4, u * sign2), (c + 6, turned * sign2)):
-                table_ref[pl.ds(step * BLOCK + 16 * t, 16)] = value
+        if odd:
+            x, y = x * cos8 + y * sin8, y * cos8 - x * sin8
+        u, v = x.astype(BF16), y.astype(BF16)
+        turned = u * real4 + v * imag4
+        for step, value in ((0, u), (2, turned), (4, u * sign2), (6, turned * sign2)):
+            table_ref[pl.ds((step + odd) * BLOCK + 16 * t, 16)] = value
 
 
 def lag_rows(ahead, behind, tail):
@@ -122,10 +129,13 @@
     lane = iota((LOCAL, 128), 1)
     ahead = jnp.where(lane <= row, tail, ahead)
     behind = jnp.where((lane >= 32) & (lane < 64 - row), tail, behind)
-    return (
-        jnp.take_along_axis(ahead, (lane + row + 1) & 127, axis=1),
-        pltpu.roll(behind, 64, 1, stride=1, stride_axis=0),
-    )
+    reverse = 7 - iota((8, 128), 0)
+    turned = []
+    for at in range(0, LOCAL, 8):
+        rows = jnp.take_along_axis(ahead[at : at + 8], reverse, axis=0)
+        rows = pltpu.roll(rows, 120 - at, 1, stride=1, stride_axis=0)
+        turned.append(jnp.take_along_axis(rows, reverse, axis=0))
+    return jnp.concatenate(turned, axis=0), pltpu.roll(behind, 64, 1, stride=1, stride_axis=0)
 
 
 def front_kernel(
@@ -149,17 +159,23 @@
     core = me % 2
     partner = me + 1 - 2 * core
     exists = lambda other: (other >= 0) & (other < ahead_count)
+    pick = lambda even, odd: jnp.where(core == 0, even, odd)
+    far = pick(-3, 3)
+    straight = lambda other: exists(other) & (other // RING == me // RING)
     barrier = pltpu.get_barrier_semaphore()
     peers = jnp.int32(1)
     pl.semaphore_signal(barrier, 1, device_id={"ch": partner}, device_id_type=MESH)
-    for step in (4, -4, 2, -2):
-        peers = peers + exists(me + step).astype(jnp.int32)
-
-        @pl.when(exists(me + step))
+    for step, there in (
+        (4, exists(me + 4)), (-4, exists(me - 4)), (far, straight(me + far)), (2, exists(me + 2)), (-2, exists(me - 2))
+    ):
+        peers = peers + there.astype(jnp.int32)
+
+        @pl.when(there)
         def _():
             pl.semaphore_signal(barrier, 1, device_id={"ch": me + step}, device_id_type=MESH)
 
-    write_table(table_ref, angle_ref, first_bin)
+    parts = table_parts(angle_ref, first_bin)
+    write_table(table_ref, angle_ref, parts, 0)
     write_spread(spread_ref)
     write_band(band_ref, (freq > 0).astype(F32), (freq < freq_count - 1).astype(F32))
 
@@ -189,8 +205,9 @@
         keep.append(lax.dot_general(usable, expand, (((0,), (0,)), ((), ())), preferred_element_type=F32))
 
     load_strain.wait()
+    write_table(table_ref, angle_ref, parts, 1)
     spectrum = jnp.zeros((ROWS, BLOCK), F32)
-    for block in range(SAMPLES // BLOCK):
+    for block in (0, 2, 4, 6, 1, 3, 5, 7):
         low = max(block * BLOCK - TIME_HALF, 0)
         high = min(block * BLOCK + BLOCK + TIME_HALF, SAMPLES)
         skip = low - (block * BLOCK - TIME_HALF)
@@ -211,19 +228,18 @@
     white_ref[...] = spectrum[:, :128] * lax.rsqrt(smooth * (1.0 / (2 * BIN_HALF + 1)) + 1e-06)
     by_window = [white_ref[pl.ds(w, LOCAL, stride=WINDOWS)] for w in range(WINDOWS)]
     lanes = iota((LOCAL, 128), 1) // 32
-    flip = (iota((LOCAL, LOCAL), 0) + iota((LOCAL, LOCAL), 1) == LOCAL - 1).astype(BF16)
+    reverse = 7 - iota((8, 128), 0)
     for group in range(GROUPS):
         for half in range(2):
             piece = None
             for i in range(4):
                 moved = pltpu.roll(by_window[4 * half + i], (32 * (i - group)) % 128, 1)
                 piece = moved if piece is None else jnp.where(lanes == i, moved, piece)
-            piece = (piece * keep[half]).astype(BF16)
+            piece = piece * keep[half]
             where = pl.ds((2 * group + half) * LOCAL, LOCAL)
-            gath_ref[SLOT_AHEAD[0], where] = piece
-            gath_ref[SLOT_BEHIND[0], where] = jnp.dot(flip, piece, preferred_element_type=F32).astype(BF16)
-
-    pick = lambda even, odd: jnp.where(core == 0, even, odd)
+            flipped = [jnp.take_along_axis(piece[at : at + 8], reverse, axis=0) for at in range(LOCAL - 8, -1, -8)]
+            gath_ref[SLOT_AHEAD[0], where] = piece.astype(BF16)
+            gath_ref[SLOT_BEHIND[0], where] = jnp.concatenate(flipped, axis=0).astype(BF16)
 
     def copy(src, dst, which, recv, target):
         return pltpu.make_async_remote_copy(
@@ -232,46 +248,53 @@
         )
 
     own_sends = [
-        (SLOT_BEHIND[0], SLOT_BEHIND[4], 7, me + 4),
-        (SLOT_AHEAD[0], SLOT_AHEAD[4], 3, me - 4),
-        (SLOT_BEHIND[0], SLOT_BEHIND[2], 5, me + 2),
-        (SLOT_AHEAD[0], SLOT_AHEAD[2], 1, me - 2),
-        (pick(SLOT_BEHIND[0], SLOT_AHEAD[0]), pick(SLOT_BEHIND[1], SLOT_AHEAD[1]), pick(4, 0), partner),
+        (SLOT_BEHIND[0], SLOT_BEHIND[4], 7, me + 4, exists(me + 4)),
+        (SLOT_AHEAD[0], SLOT_AHEAD[4], 3, me - 4, exists(me - 4)),
+        (pick(SLOT_AHEAD[0], SLOT_BEHIND[0]), pick(SLOT_AHEAD[3], SLOT_BEHIND[3]), pick(2, 6), me + far, straight(me + far)),
+        (SLOT_BEHIND[0], SLOT_BEHIND[2], 5, me + 2, exists(me + 2)),
+        (SLOT_AHEAD[0], SLOT_AHEAD[2], 1, me - 2, exists(me - 2)),
+        (pick(SLOT_BEHIND[0], SLOT_AHEAD[0]), pick(SLOT_BEHIND[1], SLOT_AHEAD[1]), pick(4, 0), partner, True),
     ]
+    own_sends = own_sends[3:5] + own_sends[:3] + own_sends[5:]
+    beyond = me + pick(4, -4)
     passes = [
-        (SLOT_BEHIND[2], pick(SLOT_BEHIND[3], SLOT_BEHIND[1]), 5, pick(6, 4), me - 2),
-        (SLOT_AHEAD[2], pick(SLOT_AHEAD[1], SLOT_AHEAD[3]), 1, pick(0, 2), me + 2),
-        (pick(SLOT_AHEAD[4], SLOT_BEHIND[4]), pick(SLOT_AHEAD[3], SLOT_BEHIND[3]), pick(3, 7), pick(2, 6), me + pick(4, -4)),
+        (SLOT_BEHIND[2], pick(SLOT_BEHIND[3], SLOT_BEHIND[1]), 5, pick(6, 4), exists(me - 2)),
+        (SLOT_AHEAD[2], pick(SLOT_AHEAD[1], SLOT_AHEAD[3]), 1, pick(0, 2), exists(me + 2)),
+        (
+            pick(SLOT_AHEAD[4], SLOT_BEHIND[4]), pick(SLOT_AHEAD[3], SLOT_BEHIND[3]), pick(3, 7), pick(2, 6),
+            exists(beyond) & ~straight(beyond),
+        ),
     ]
     pl.semaphore_wait(barrier, peers)
-    for which, (src, dst, recv, target) in enumerate(own_sends):
-        @pl.when(exists(target))
+    for which, (src, dst, recv, target, there) in enumerate(own_sends):
+        @pl.when(there)
         def _():
             copy(src, dst, which, recv, target).start()
-    for i, (src, dst, mine, recv, source) in enumerate(passes):
-        @pl.when(exists(source))
+    for i, (src, dst, mine, recv, there) in enumerate(passes):
+        @pl.when(there)
         def _():
             copy(src, src, 0, mine, partner).wait_recv()
-            copy(src, dst, 5 + i, recv, partner).start()
-
-    for slot, mine, source in (
-        (pick(SLOT_BEHIND[4], SLOT_AHEAD[4]), pick(7, 3), me - pick(4, -4)),
-        (pick(SLOT_AHEAD[1], SLOT_BEHIND[1]), pick(0, 4), partner),
-        (pick(SLOT_BEHIND[1], SLOT_AHEAD[1]), pick(4, 0), me - pick(1, -1)),
-        (SLOT_AHEAD[3], 2, me + 3),
-        (SLOT_BEHIND[3], 6, me - 3),
+            copy(src, dst, 6 + i, recv, partner).start()
+
+    for slot, mine, there in (
+        (pick(SLOT_AHEAD[4], SLOT_BEHIND[4]), pick(3, 7), straight(beyond)),
+        (pick(SLOT_BEHIND[4], SLOT_AHEAD[4]), pick(7, 3), exists(me - pick(4, -4))),
+        (pick(SLOT_AHEAD[1], SLOT_BEHIND[1]), pick(0, 4), True),
+        (pick(SLOT_BEHIND[1], SLOT_AHEAD[1]), pick(4, 0), exists(me - pick(1, -1))),
+        (SLOT_AHEAD[3], 2, exists(me + 3)),
+        (SLOT_BEHIND[3], 6, exists(me - 3)),
     ):
-        @pl.when(exists(source))
+        @pl.when(there)
         def _():
             copy(slot, slot, 0, mine, partner).wait_recv()
-    for which, (src, dst, recv, target) in enumerate(own_sends):
-        @pl.when(exists(target))
+    for which, (src, dst, recv, target, there) in enumerate(own_sends):
+        @pl.when(there)
         def _():
             copy(src, dst, which, recv, target).wait_send()
-    for i, (src, dst, mine, recv, source) in enumerate(passes):
-        @pl.when(exists(source))
-        def _():
-            copy(src, dst, 5 + i, recv, partner).wait_send()
+    for i, (src, dst, mine, recv, there) in enumerate(passes):
+        @pl.when(there)
+        def _():
+            copy(src, dst, 6 + i, recv, partner).wait_send()
 
 
 def front(strain, channel_ok, window_ok, ahead_count, freq_count):
@@ -288,13 +311,13 @@
             pltpu.VMEM((1, LOCAL), jnp.int32),
             pltpu.VMEM((WINDOWS, LOCAL), jnp.int32),
             pltpu.VMEM((SAMPLES, BLOCK), BF16),
-            pltpu.VMEM((2, 40, BLOCK), F32),
+            pltpu.VMEM((2, 32, BLOCK), F32),
             pltpu.VMEM((2 * BLOCK, BLOCK), BF16),
             pltpu.VMEM((BLOCK, 128), BF16),
             pltpu.VMEM((ROWS, 128), F32),
             pltpu.SemaphoreType.DMA,
             pltpu.SemaphoreType.DMA((2,)),
-            pltpu.SemaphoreType.DMA((8,)),
+            pltpu.SemaphoreType.DMA((9,)),
             pltpu.SemaphoreType.DMA((8,)),
         ],
         compiler_params=pltpu.CompilerParams(collective_id=0, has_side_effects=True, vmem_limit_bytes=VMEM_LIMIT),
@@ -339,10 +362,12 @@
                 ahead, behind = lag_rows(cross[rows, :128], cross[rows, 128:256], cross[rows, 256:])
                 ahead_ref[part, step * per_step + f] = (ahead * scales[0]).astype(BF16)
                 behind_ref[part, step * per_step + f] = (behind * scales[1]).astype(BF16)
-        done = pl.ds(step * per_step, per_step)
-        for side, (src, dst) in enumerate(((ahead_ref, ahead_hbm), (behind_ref, behind_hbm))):
-            copies.append(pltpu.make_async_copy(src.at[:, done], dst.at[:, done], out_sem.at[side, step]))
-            copies[-1].start()
+            done = pl.ds(step * per_step, per_step)
+            for side, (src, dst) in enumerate(((ahead_ref, ahead_hbm), (behind_ref, behind_hbm))):
+                copies.append(
+                    pltpu.make_async_copy(src.at[part, done], dst.at[part, done], out_sem.at[side, part, step])
+                )
+                copies[-1].start()
     for copy in copies:
         copy.wait()
 
@@ -356,7 +381,7 @@
         out_shape=(jax.ShapeDtypeStruct(shape, BF16), jax.ShapeDtypeStruct(shape, BF16)),
         in_specs=[vmem],
         out_specs=(hbm, hbm),
-        scratch_shapes=[pltpu.VMEM(shape, BF16), pltpu.VMEM(shape, BF16), pltpu.SemaphoreType.DMA((2, STEPS))],
+        scratch_shapes=[pltpu.VMEM(shape, BF16), pltpu.VMEM(shape, BF16), pltpu.SemaphoreType.DMA((2, 2, STEPS))],
         compiler_params=pltpu.CompilerParams(vmem_limit_bytes=VMEM_LIMIT),
         name="cross",
     )(gathered)

time: 16.4 us -> 15.8 us (0.963)
  the two profiles are of different devices: /device:TPU:189 before, /device:TPU:191 now
where the time goes in v4:
time: 15.8 us; the launch traced here: 15.6 us
  Pallas kernels  15 us (95%)
  between operations  0.64 us (4%)
    pallas_call x1, Pallas kernels, front(): pl.pallas_call(functools.partial(front_kernel, ahead_count, freq_count),...  13.3 us
    pallas_call x1, Pallas kernels, cross(): pl.pallas_call(cross_kernel, out_shape=(jax.ShapeDtypeStruct(shape, BF16)...  1.68 us

profile of v4, /device:TPU:191, one launch (start us, length us, event | category | flops | bytes accessed | tf_op | source)
XLA Modules:
  0.0 15.6 jit_solution(7493768267101685144)
XLA Ops:
  0.6 13.3 %front.1.gath_ref = bf16[12,136,128]{2,1,0:T(8,128)(2,1)S(1)} custom-call(bf16[256,2048]{1,0:T(8,128)(2,1)} %bitcast.3, s32[1,32]{1,0:T(1,128)} %bitcast.5, s32[8,32]{1,0:T(8,128)} %bitcast.4), custom_call_target="tpu_custom_call" | custom-call | tf_op jit(solution)/shard_map/front/pallas_call | solution.py:304
  13.9 1.7 %cross.1 = (bf16[2,32,32,128]{3,2,1,0:T(8,128)(2,1)}, bf16[2,32,32,128]{3,2,1,0:T(8,128)(2,1)}) custom-call(bf16[12,136,128]{2,1,0:T(8,128)(2,1)S(1)} %front.1.gath_ref), custom_call_target="tpu_custom_call" | custom-call | tf_op jit(solution)/shard_map/cross/pallas_call | solution.py:379

commit v5 on v4

--- a/solution.py
+++ b/solution.py
@@ -176,6 +176,7 @@
 
     parts = table_parts(angle_ref, first_bin)
     write_table(table_ref, angle_ref, parts, 0)
+    write_table(table_ref, angle_ref, parts, 1)
     write_spread(spread_ref)
     write_band(band_ref, (freq > 0).astype(F32), (freq < freq_count - 1).astype(F32))
 
@@ -205,9 +206,7 @@
         keep.append(lax.dot_general(usable, expand, (((0,), (0,)), ((), ())), preferred_element_type=F32))
 
     load_strain.wait()
-    write_table(table_ref, angle_ref, parts, 1)
-    spectrum = jnp.zeros((ROWS, BLOCK), F32)
-    for block in (0, 2, 4, 6, 1, 3, 5, 7):
+    def leveled(block):
         low = max(block * BLOCK - TIME_HALF, 0)
         high = min(block * BLOCK + BLOCK + TIME_HALF, SAMPLES)
         skip = low - (block * BLOCK - TIME_HALF)
@@ -215,16 +214,16 @@
             jnp.abs(x_ref[:, low:high]), spread_ref[skip : skip + high - low], preferred_element_type=F32
         )
         level = sums * (1.0 / (2 * TIME_HALF + 1)) + 1e-06
-        leveled = (x_ref[:, block * BLOCK : (block + 1) * BLOCK].astype(F32) / level).astype(BF16)
+        return (x_ref[:, block * BLOCK : (block + 1) * BLOCK].astype(F32) / level).astype(BF16)
+
+    spectrum = jnp.zeros((ROWS, BLOCK), F32)
+    for first in (0, 2, 4, 6):
+        both = jnp.concatenate([leveled(first), leveled(first + 1)], axis=1)
         spectrum = spectrum + jnp.dot(
-            leveled, table_ref[block * BLOCK : (block + 1) * BLOCK], preferred_element_type=F32
+            both, table_ref[first * BLOCK : (first + 2) * BLOCK], preferred_element_type=F32
         )
     power = spectrum * spectrum
-    coarse = power.astype(BF16)
-    fine = (power - coarse.astype(F32)).astype(BF16)
-    smooth = jnp.dot(coarse, band_ref[...], preferred_element_type=F32) + jnp.dot(
-        fine, band_ref[...], preferred_element_type=F32
-    )
+    smooth = jnp.dot(power.astype(BF16), band_ref[...], preferred_element_type=F32)
     white_ref[...] = spectrum[:, :128] * lax.rsqrt(smooth * (1.0 / (2 * BIN_HALF + 1)) + 1e-06)
     by_window = [white_ref[pl.ds(w, LOCAL, stride=WINDOWS)] for w in range(WINDOWS)]
     lanes = iota((LOCAL, 128), 1) // 32

time: 15.8 us -> 15.8 us (level)
  no operation moved by 1% of the time
where the time goes in v5:
time: 15.8 us; the launch traced here: 15.6 us
  Pallas kernels  15 us (95%)
  between operations  0.64 us (4%)
    pallas_call x1, Pallas kernels, front(): pl.pallas_call(functools.partial(front_kernel, ahead_count, freq_count),...  13.3 us
    pallas_call x1, Pallas kernels, cross(): pl.pallas_call(cross_kernel, out_shape=(jax.ShapeDtypeStruct(shape, BF16)...  1.68 us

profile of v5, /device:TPU:191, one launch (start us, length us, event | category | flops | bytes accessed | tf_op | source)
XLA Modules:
  0.0 15.6 jit_solution(8097307148968712943)
XLA Ops:
  0.6 13.3 %front.1.gath_ref = bf16[12,136,128]{2,1,0:T(8,128)(2,1)S(1)} custom-call(bf16[256,2048]{1,0:T(8,128)(2,1)} %bitcast.3, s32[1,32]{1,0:T(1,128)} %bitcast.5, s32[8,32]{1,0:T(8,128)} %bitcast.4), custom_call_target="tpu_custom_call" | custom-call | tf_op jit(solution)/shard_map/front/pallas_call | solution.py:303
  13.9 1.7 %cross.1 = (bf16[2,32,32,128]{3,2,1,0:T(8,128)(2,1)}, bf16[2,32,32,128]{3,2,1,0:T(8,128)(2,1)}) custom-call(bf16[12,136,128]{2,1,0:T(8,128)(2,1)S(1)} %front.1.gath_ref), custom_call_target="tpu_custom_call" | custom-call | tf_op jit(solution)/shard_map/cross/pallas_call | solution.py:378

commit v6 on v5

--- a/solution.py
+++ b/solution.py
@@ -223,7 +223,11 @@
             both, table_ref[first * BLOCK : (first + 2) * BLOCK], preferred_element_type=F32
         )
     power = spectrum * spectrum
-    smooth = jnp.dot(power.astype(BF16), band_ref[...], preferred_element_type=F32)
+    coarse = power.astype(BF16)
+    fine = (power - coarse.astype(F32)).astype(BF16)
+    smooth = jnp.dot(coarse, band_ref[...], preferred_element_type=F32) + jnp.dot(
+        fine, band_ref[...], preferred_element_type=F32
+    )
     white_ref[...] = spectrum[:, :128] * lax.rsqrt(smooth * (1.0 / (2 * BIN_HALF + 1)) + 1e-06)
     by_window = [white_ref[pl.ds(w, LOCAL, stride=WINDOWS)] for w in range(WINDOWS)]
     lanes = iota((LOCAL, 128), 1) // 32

time: 15.8 us -> 15.8 us (level)
  no operation moved by 1% of the time
where the time goes in v6:
time: 15.8 us; the launch traced here: 15.6 us
  Pallas kernels  15 us (95%)
  between operations  0.64 us (4%)
    pallas_call x1, Pallas kernels, front(): pl.pallas_call(functools.partial(front_kernel, ahead_count, freq_count),...  13.3 us
    pallas_call x1, Pallas kernels, cross(): pl.pallas_call(cross_kernel, out_shape=(jax.ShapeDtypeStruct(shape, BF16)...  1.68 us

profile of v6, /device:TPU:191, one launch (start us, length us, event | category | flops | bytes accessed | tf_op | source)
XLA Modules:
  0.0 15.6 jit_solution(7454316433386986436)
XLA Ops:
  0.6 13.3 %front.1.gath_ref = bf16[12,136,128]{2,1,0:T(8,128)(2,1)S(1)} custom-call(bf16[256,2048]{1,0:T(8,128)(2,1)} %bitcast.3, s32[1,32]{1,0:T(1,128)} %bitcast.5, s32[8,32]{1,0:T(8,128)} %bitcast.4), custom_call_target="tpu_custom_call" | custom-call | tf_op jit(solution)/shard_map/front/pallas_call | solution.py:307
  13.9 1.7 %cross.1 = (bf16[2,32,32,128]{3,2,1,0:T(8,128)(2,1)}, bf16[2,32,32,128]{3,2,1,0:T(8,128)(2,1)}) custom-call(bf16[12,136,128]{2,1,0:T(8,128)(2,1)S(1)} %front.1.gath_ref), custom_call_target="tpu_custom_call" | custom-call | tf_op jit(solution)/shard_map/cross/pallas_call | solution.py:382
